TPU v7x, 128 devices: a whole 4x4x4 slice. The times are simulated.
128 devices in a mesh: chan: 8 (over x, core), row: 16 (over y, z).
Axes of the slice: x: 4, y: 4, z: 4, core: 2. Of those that a mesh axis runs over, the one named last changes fastest.
Arguments:
- generator: bfloat16 [8, 2560, 2560], P('chan', 'row'), may hold values from -0.06 to 0.06, as said below
- hamiltonian: bfloat16 [8, 2560, 2560], P('chan', 'row'), may hold values from -6 to 6, as said below
- live_states: int32 [8], P('chan'), may hold values from 1 to 2560, 11520 in all
- pp_occupation: int32 [8, 2560], P('chan'), may hold values from -1 to 1
- ph_occupation: int32 [8, 2560], P('chan'), may hold values from -1 to 1
- ph_order: int32 [8, 2560], P('chan'), may hold values from 0 to 2559, as said below
- recoupling: float32 [8, 2], replicated, may hold values from 0.4 to 1
Outputs:
- transformed: float32 [8, 2560, 2560], P('chan', 'row')
Inputs may be any that keep to these rules, and one draw needn't show every extreme that they name: Each generator[c] is antisymmetric. Each hamiltonian[c] is symmetric. Each ph_order[c] is a permutation of 0 to 2559, and entry r * 160 + q * 16 + s, for 0 <= q < 10, lies in [s * 160, (s + 1) * 160).
All inputs are finite; a program needn't handle non-finite values. No bound on the sum of `live_states` on one device may be relied on, other than what follows from the above.
Results may differ from a plain program's by a relative error of at most 0.005.
Values may be sent and summed in bfloat16 or wider, within the bound.
No kernel may reach another device: no remote copies, remote signals or barrier semaphores. Data moves between devices by JAX's collectives and lax.ppermute only.
A program may use at most 128 MiB of HBM per device.

v0:
```python
import jax
import jax.numpy as jnp
from jax import lax
from jax.sharding import PartitionSpec as P

TERMS = 3


def swapped(value, axis, apart):
    return lax.ppermute(value, axis, [(i, i ^ 1 << apart) for i in range(lax.axis_size(axis))])


def on_device(
    generator, hamiltonian, live_states, pp_occupation, ph_occupation, ph_order, recoupling
):
    row_count = generator.shape[1]
    state_count = generator.shape[2]
    shard_count = lax.axis_size("row")
    my_shard = lax.axis_index("row")
    top_bit = lax.axis_size("chan").bit_length() - 2
    my_group = lax.axis_index("chan")
    partner = jnp.bitwise_xor(my_group, lax.axis_size("chan") // 2)
    own_weights = recoupling[my_group]
    partner_weights = recoupling[partner]
    fanout = row_count // shard_count
    positions = jnp.arange(state_count, dtype=jnp.int32)
    live_count = live_states[0]
    column_alive = positions < live_count
    row_alive = my_shard * row_count + jnp.arange(row_count, dtype=jnp.int32) < live_count
    block_alive = row_alive[:, None] & column_alive[None, :]
    channel_order = ph_order[0]
    inverse = jnp.zeros((state_count,), jnp.int32).at[channel_order].set(positions)
    pp_weights = jnp.where(column_alive, pp_occupation[0], 0).astype(jnp.bfloat16)
    ph_weights = jnp.where(column_alive, ph_occupation[0][inverse], 0).astype(jnp.bfloat16)
    order_cube = channel_order.reshape(shard_count, fanout, shard_count)
    send_rows = (
        lax.dynamic_index_in_dim(order_cube, my_shard, 2, keepdims=False) - my_shard * row_count
    )
    send_order = send_rows.T.reshape(row_count)
    back_order = (
        jnp.zeros((row_count,), jnp.int32)
        .at[send_order]
        .set(jnp.arange(row_count, dtype=jnp.int32))
    )
    own_share = jnp.where(block_alive, generator[0], jnp.zeros_like(generator[0]))
    partner_share = swapped(own_share, "chan", top_bit)
    full_own, full_partner = (
        lax.all_gather(own_share, "row", axis=0, tiled=True),
        lax.all_gather(partner_share, "row", axis=0, tiled=True),
    )
    current = jnp.where(block_alive, hamiltonian[0], jnp.zeros_like(hamiltonian[0]))
    running = current.astype(jnp.float32)
    for term_index in range(1, TERMS + 1):
        masked = current * pp_weights[None, :]
        pp_prod = jnp.dot(masked, full_own, preferred_element_type=jnp.float32).astype(jnp.bfloat16)
        partner_rows = swapped(current, "chan", top_bit)
        mixed = (
            own_weights[0] * current.astype(jnp.float32)
            + own_weights[1] * partner_rows.astype(jnp.float32)
        ).astype(jnp.bfloat16)
        outgoing = mixed[send_order].reshape(fanout, shard_count, state_count)
        recoupled = lax.all_to_all(
            outgoing, "row", split_axis=1, concat_axis=1, tiled=True
        ).reshape(row_count, state_count)
        weighted = recoupled * ph_weights[None, :]
        near_part = jnp.dot(weighted, full_own, preferred_element_type=jnp.float32)
        far_part = jnp.dot(weighted, full_partner, preferred_element_type=jnp.float32)
        ph_prod = (own_weights[0] * near_part + own_weights[1] * far_part).astype(jnp.bfloat16)
        arrived = lax.all_to_all(
            ph_prod.reshape(fanout, shard_count, state_count),
            "row",
            split_axis=1,
            concat_axis=1,
            tiled=True,
        )
        returned = arrived.reshape(row_count, state_count)[back_order]
        partner_back = swapped(returned, "chan", top_bit)
        combined = (
            pp_prod.astype(jnp.float32)
            + own_weights[0] * returned.astype(jnp.float32)
            + partner_weights[1] * partner_back.astype(jnp.float32)
        ).astype(jnp.bfloat16)
        flipped = lax.all_to_all(combined, "row", split_axis=1, concat_axis=0, tiled=True).T
        increment = -(combined.astype(jnp.float32) + flipped.astype(jnp.float32)) / term_index
        running = running + increment
        current = increment.astype(jnp.bfloat16)
    return running[None]


def solution(mesh):
    placed = (
        P("chan", "row", None),
        P("chan", "row", None),
        P("chan"),
        P("chan", None),
        P("chan", None),
        P("chan", None),
        P(),
    )
    return jax.shard_map(
        on_device, mesh=mesh, in_specs=placed, out_specs=P("chan", "row", None), check_vma=False
    )
```

profile of v0, /device:TPU:0, one launch (start us, length us, event | category | flops | bytes accessed | tf_op | source)
XLA Modules:
  0.0 565.1 jit_solution(3157261852502357082)
XLA Ops:
  13.3 18.5 %collective-permute-done.1 = bf16[160,2560]{1,0:T(8,128)(2,1)S(1)} collective-permute-done((bf16[160,2560]{1,0:T(8,128)(2,1)}, bf16[160,2560]{1,0:T(8,128)(2,1)S(1)}, u32[]{:S(2)}, u32[]{:S(2)}) %collective-permute-start.1) | collective-permute-done | bytes 819232 | tf_op jit(solution)/shard_map/ppermute | solution.py:10
  37.4 16.1 %collective-permute-done = bf16[160,2560]{1,0:T(8,128)(2,1)S(1)} collective-permute-done((bf16[160,2560]{1,0:T(8,128)(2,1)S(1)}, bf16[160,2560]{1,0:T(8,128)(2,1)S(1)}, u32[]{:S(2)}, u32[]{:S(2)}) %collective-permute-start) | collective-permute-done | bytes 819232 | tf_op jit(solution)/shard_map/ppermute | solution.py:10
  66.0 9.9 %scatter_custom_fusion = s32[2560]{0:T(1024)S(1)} fusion(s32[2560]{0:T(1024)S(1)} %fusion.30, s32[2560]{0:T(1024)S(1)} %iota.23, s32[]{:T(128)} %constant.15.clone.1), kind=kCustom, calls=%fused_computation.74 | custom fusion | bytes 10244 | tf_op jit(solution)/shard_map/scatter | solution.py:32
  75.9 13.6 %gather_fusion.1 = s32[2560]{0:T(1024)S(1)} fusion(s32[2560]{0:T(1024)S(1)} %reduce.3, s32[3072]{0:T(1024)S(1)} %pad_clamp_fusion), kind=kCustom, calls=%fused_computation.1 | custom fusion | bytes 30720 | tf_op jit(solution)/shard_map/gather | solution.py:34
  97.0 22.3 %all-gather.3.cloned.1.call-done = bf16[2560,2560]{1,0:T(8,128)(2,1)} async-done(((bf16[160,2560]{1,0:T(8,128)(2,1)}), bf16[2560,2560]{1,0:T(8,128)(2,1)}) %all-gather.3.cloned.1.call-update) | async-done | bytes 13107216 | tf_op jit(solution)/shard_map/all_gather | solution.py:48
  127.0 86.6 %all-gather.5.cloned.1.call-done = bf16[2560,2560]{1,0:T(8,128)(2,1)} async-done(((bf16[160,2560]{1,0:T(8,128)(2,1)}), bf16[2560,2560]{1,0:T(8,128)(2,1)}) %all-gather.5.cloned.1.call-update) | async-done | bytes 13107216 | tf_op jit(solution)/shard_map/all_gather | solution.py:49
  229.3 19.5 %all-to-all-done.1 = bf16[10,16,2560]{2,0,1:T(8,128)(2,1)S(1)} async-done(((bf16[10,16,2560]{2,0,1:T(8,128)(2,1)}), bf16[10,16,2560]{2,0,1:T(8,128)(2,1)S(1)}, u32[]{:S(2)}, u32[]{:S(2)}) %all-to-all-start.1) | async-done | bytes 819232 | tf_op jit(solution)/shard_map/all_to_all | solution.py:69
  254.2 15.1 %collective-permute-done.2 = bf16[160,2560]{1,0:T(8,128)(2,1)S(1)} collective-permute-done((bf16[160,2560]{1,0:T(8,128)(2,1)S(1)}, bf16[160,2560]{1,0:T(8,128)(2,1)S(1)}, u32[]{:S(2)}, u32[]{:S(2)}) %collective-permute-start.2) | collective-permute-done | bytes 819232 | tf_op jit(solution)/shard_map/ppermute | solution.py:10
  269.3 8.4 %add_convert_fusion.4 = bf16[160,2560]{1,0:T(8,128)(2,1)S(1)} fusion(bf16[160,2560]{1,0:T(8,128)(2,1)S(1)} %collective-permute-done.2, bf16[2560,2560]{1,0:T(8,128)(2,1)} %all-gather.3.cloned.1.call-done, bf16[160,2560]{1,0:T(8,128)(2,1)S(1)} %gather_fusion.2, f32[]{:T(128)} %bitcast.12, f32[]{:T(128)} %bitcast.3, ...), kind=kOutput, calls=%fused_computation.52 | convolution fusion | flops 2101248000 | bytes 16389128 | tf_op jit(solution)/shard_map/dot_general | solution.py:55
  279.8 22.0 %all_to_all.69 = bf16[160,16,160]{2,0,1:T(8,128)(2,1)S(1)} all-to-all(bf16[160,16,160]{2,0,1:T(8,128)(2,1)S(1)} %copy.36), channel_id=1, replica_groups=mesh['chan'=8,'row'=16] {'row'}, dimensions={1} | all-to-all | bytes 1638400 | tf_op jit(solution)/shard_map/all_to_all | solution.py:83
  309.0 14.9 %collective-permute-done.3 = bf16[160,2560]{1,0:T(8,128)(2,1)S(1)} collective-permute-done((bf16[160,2560]{1,0:T(8,128)(2,1)S(1)}, bf16[160,2560]{1,0:T(8,128)(2,1)S(1)}, u32[]{:S(2)}, u32[]{:S(2)}) %collective-permute-start.3) | collective-permute-done | bytes 819232 | tf_op jit(solution)/shard_map/ppermute | solution.py:10
  329.2 19.8 %all_to_all.70 = bf16[10,16,2560]{2,0,1:T(8,128)(2,1)S(1)} all-to-all(bf16[10,16,2560]{2,0,1:T(8,128)(2,1)S(1)} %copy.38), channel_id=1, replica_groups=mesh['chan'=8,'row'=16] {'row'}, dimensions={1} | all-to-all | bytes 1638400 | tf_op jit(solution)/shard_map/all_to_all | solution.py:62
  349.6 8.3 %convolution_multiply_fusion.3 = f32[160,2560]{1,0:T(8,128)S(1)} fusion(bf16[160,2560]{1,0:T(8,128)(2,1)S(1)} %bitcast_multiply_fusion.1, bf16[2560,2560]{1,0:T(8,128)(2,1)} %all-gather.3.cloned.1.call-done, f32[]{:T(128)} %bitcast.3), kind=kOutput, calls=%fused_computation.12 | convolution fusion | flops 2097561600 | bytes 15564804 | tf_op jit(solution)/shard_map/dot_general | solution.py:66
  361.3 18.1 %all_to_all.71 = bf16[10,16,2560]{2,0,1:T(8,128)(2,1)S(1)} all-to-all(bf16[10,16,2560]{2,0,1:T(8,128)(2,1)S(1)} %copy.40), channel_id=1, replica_groups=mesh['chan'=8,'row'=16] {'row'}, dimensions={1} | all-to-all | bytes 1638400 | tf_op jit(solution)/shard_map/all_to_all | solution.py:69
  385.1 12.0 %collective-permute-done.4 = bf16[160,2560]{1,0:T(8,128)(2,1)S(1)} collective-permute-done((bf16[160,2560]{1,0:T(8,128)(2,1)}, bf16[160,2560]{1,0:T(8,128)(2,1)S(1)}, u32[]{:S(2)}, u32[]{:S(2)}) %collective-permute-start.4) | collective-permute-done | bytes 819232 | tf_op jit(solution)/shard_map/ppermute | solution.py:10
  397.2 8.7 %add_convert_fusion.2 = bf16[160,2560]{1,0:T(8,128)(2,1)S(1)} fusion(bf16[160,2560]{1,0:T(8,128)(2,1)S(1)} %collective-permute-done.4, bf16[2560,2560]{1,0:T(8,128)(2,1)} %all-gather.3.cloned.1.call-done, bf16[160,2560]{1,0:T(8,128)(2,1)} %gather_fusion.4, bf16[160,2560]{1,0:T(8,128)(2,1)} %copy-done.7, f32[]{:T(128)} %bitcast.12, f32[]{:T(128)} %bitcast.3, ...), kind=kOutput, calls=%fused_computation.50 | convolution fusion | flops 2101248000 | bytes 16389128 | tf_op jit(solution)/shard_map/dot_general | solution.py:55
  407.3 18.2 %all_to_all.72 = bf16[160,16,160]{0,2,1:T(8,128)(2,1)S(1)} all-to-all(bf16[160,16,160]{0,2,1:T(8,128)(2,1)} %bitcast.96), channel_id=1, replica_groups=mesh['chan'=8,'row'=16] {'row'}, dimensions={1} | all-to-all | bytes 1638400 | tf_op jit(solution)/shard_map/all_to_all | solution.py:83
  437.6 10.8 %collective-permute-done.5 = bf16[160,2560]{1,0:T(8,128)(2,1)S(1)} collective-permute-done((bf16[160,2560]{1,0:T(8,128)(2,1)S(1)}, bf16[160,2560]{1,0:T(8,128)(2,1)S(1)}, u32[]{:S(2)}, u32[]{:S(2)}) %collective-permute-start.5) | collective-permute-done | bytes 819232 | tf_op jit(solution)/shard_map/ppermute | solution.py:10
  453.7 17.6 %all_to_all.73 = bf16[10,16,2560]{2,0,1:T(8,128)(2,1)S(1)} all-to-all(bf16[10,16,2560]{2,0,1:T(8,128)(2,1)S(1)} %copy.44), channel_id=1, replica_groups=mesh['chan'=8,'row'=16] {'row'}, dimensions={1} | all-to-all | bytes 1638400 | tf_op jit(solution)/shard_map/all_to_all | solution.py:62
  471.9 8.3 %convolution_multiply_fusion.1 = f32[160,2560]{1,0:T(8,128)S(1)} fusion(bf16[160,2560]{1,0:T(8,128)(2,1)S(1)} %bitcast_multiply_fusion, bf16[2560,2560]{1,0:T(8,128)(2,1)} %all-gather.3.cloned.1.call-done, f32[]{:T(128)} %bitcast.3), kind=kOutput, calls=%fused_computation.10 | convolution fusion | flops 2097561600 | bytes 15564804 | tf_op jit(solution)/shard_map/dot_general | solution.py:66
  483.6 17.8 %all_to_all.74 = bf16[10,16,2560]{2,0,1:T(8,128)(2,1)S(1)} all-to-all(bf16[10,16,2560]{2,0,1:T(8,128)(2,1)S(1)} %copy.46), channel_id=1, replica_groups=mesh['chan'=8,'row'=16] {'row'}, dimensions={1} | all-to-all | bytes 1638400 | tf_op jit(solution)/shard_map/all_to_all | solution.py:69
  506.9 11.0 %collective-permute-done.6 = bf16[160,2560]{1,0:T(8,128)(2,1)S(1)} collective-permute-done((bf16[160,2560]{1,0:T(8,128)(2,1)}, bf16[160,2560]{1,0:T(8,128)(2,1)S(1)}, u32[]{:S(2)}, u32[]{:S(2)}) %collective-permute-start.6) | collective-permute-done | bytes 819232 | tf_op jit(solution)/shard_map/ppermute | solution.py:10
  517.9 9.6 %add_convert_fusion = bf16[160,2560]{1,0:T(8,128)(2,1)} fusion(bf16[160,2560]{1,0:T(8,128)(2,1)S(1)} %collective-permute-done.6, bf16[2560,2560]{1,0:T(8,128)(2,1)} %all-gather.3.cloned.1.call-done, bf16[160,2560]{1,0:T(8,128)(2,1)} %gather_fusion.6, bf16[160,2560]{1,0:T(8,128)(2,1)} %copy-done.6, f32[]{:T(128)} %bitcast.12, f32[]{:T(128)} %bitcast.3, ...), kind=kOutput, calls=%fused_computation.48 | convolution fusion | flops 2101248000 | bytes 16389128 | tf_op jit(solution)/shard_map/dot_general | solution.py:55
  530.6 17.6 %all_to_all.75 = bf16[160,16,160]{2,0,1:T(8,128)(2,1)S(1)} all-to-all(bf16[160,16,160]{2,0,1:T(8,128)(2,1)S(1)} %copy.48), channel_id=1, replica_groups=mesh['chan'=8,'row'=16] {'row'}, dimensions={1} | all-to-all | bytes 1638400 | tf_op jit(solution)/shard_map/all_to_all | solution.py:83
  (123 shorter events, 125.2 us)
Async XLA Ops:
  6.5 59.3 %copy-start = (s32[1,2560]{1,0:T(1,128)S(1)}, s32[1,2560]{1,0:T(1,128)}, u32[]{:S(2)}) copy-start(s32[1,2560]{1,0:T(1,128)} %param.11) | copy-start | bytes 30724
  6.5 112.8 %all-gather.3.cloned.1.call-start = ((), (), s32[]{:S(2)}) async-start(), calls=%async_computation.9 | async-start | bytes 13926400 | tf_op jit(solution)/shard_map/all_gather | solution.py:48
  10.0 259.3 %copy-start.2 = (bf16[160,2560]{1,0:T(8,128)(2,1)}, bf16[160,2560]{1,0:T(8,128)(2,1)S(1)}, u32[]{:S(2)}) copy-start(bf16[160,2560]{1,0:T(8,128)(2,1)S(1)} %get-tuple-element.6) | copy-start | bytes 2457604
  10.0 26.0 %copy-start.9 = (s32[1,2560]{1,0:T(1,128)S(1)}, s32[1,2560]{1,0:T(1,128)}, u32[]{:S(2)}) copy-start(s32[1,2560]{1,0:T(1,128)} %param.12) | copy-start | bytes 30724
  10.0 26.7 %copy-start.11 = (f32[8,2]{0,1:T(2,128)S(1)}, f32[8,2]{0,1:T(2,128)}, u32[]{:S(2)}) copy-start(f32[8,2]{0,1:T(2,128)} %param.13) | copy-start | bytes 196
  10.0 203.6 %all-gather.5.cloned.1.call-start = ((), (), s32[]{:S(2)}) async-start(), calls=%async_computation.10 | async-start | bytes 13926400 | tf_op jit(solution)/shard_map/all_gather | solution.py:49
  10.1 21.7 %collective-permute-start.1 = (bf16[160,2560]{1,0:T(8,128)(2,1)}, bf16[160,2560]{1,0:T(8,128)(2,1)S(1)}, u32[]{:S(2)}, u32[]{:S(2)}) collective-permute-start(bf16[160,2560]{1,0:T(8,128)(2,1)} %get-tuple-element.5), channel_id=1, source_target_pairs={{0,64},{16,80},{32,96},{48,112},{64,0},{80,16},{96,32},{112,48},{1... | collective-permute-start | bytes 2457608 | tf_op jit(solution)/shard_map/ppermute | solution.py:10
  32.7 20.8 %collective-permute-start = (bf16[160,2560]{1,0:T(8,128)(2,1)S(1)}, bf16[160,2560]{1,0:T(8,128)(2,1)S(1)}, u32[]{:S(2)}, u32[]{:S(2)}) collective-permute-start(bf16[160,2560]{1,0:T(8,128)(2,1)S(1)} %get-tuple-element.6), channel_id=1, source_target_pairs={{0,64},{16,80},{32,96},{48,112},{64,0},{80,16},{96,32},{112,48},{1... | collective-permute-start | bytes 2457608 | tf_op jit(solution)/shard_map/ppermute | solution.py:10
  57.7 38.7 %all-to-all-start = ((bf16[10,16,2560]{2,0,1:T(8,128)(2,1)}), bf16[10,16,2560]{2,0,1:T(8,128)(2,1)S(1)}, u32[]{:S(2)}, u32[]{:S(2)}) async-start(bf16[10,16,2560]{2,0,1:T(8,128)(2,1)} %copy.32), calls=%async_computation | async-start | bytes 2621440 | tf_op jit(solution)/shard_map/all_to_all | solution.py:62
  222.9 25.9 %all-to-all-start.1 = ((bf16[10,16,2560]{2,0,1:T(8,128)(2,1)}), bf16[10,16,2560]{2,0,1:T(8,128)(2,1)S(1)}, u32[]{:S(2)}, u32[]{:S(2)}) async-start(bf16[10,16,2560]{2,0,1:T(8,128)(2,1)} %copy.34), calls=%async_computation.1 | async-start | bytes 2621440 | tf_op jit(solution)/shard_map/all_to_all | solution.py:69
  250.4 18.9 %collective-permute-start.2 = (bf16[160,2560]{1,0:T(8,128)(2,1)S(1)}, bf16[160,2560]{1,0:T(8,128)(2,1)S(1)}, u32[]{:S(2)}, u32[]{:S(2)}) collective-permute-start(bf16[160,2560]{1,0:T(8,128)(2,1)S(1)} %gather_fusion.2), channel_id=1, source_target_pairs={{0,64},{16,80},{32,96},{48,112},{64,0},{80,16},{96,32},{112,48},{1... | collective-permute-start | bytes 2457608 | tf_op jit(solution)/shard_map/ppermute | solution.py:10
  277.7 28.0 %copy-start.4 = (bf16[160,2560]{1,0:T(8,128)(2,1)}, bf16[160,2560]{1,0:T(8,128)(2,1)S(1)}, u32[]{:S(2)}) copy-start(bf16[160,2560]{1,0:T(8,128)(2,1)S(1)} %add_convert_fusion.4) | copy-start | bytes 2457604
  305.9 18.0 %copy-start.7 = (bf16[160,2560]{1,0:T(8,128)(2,1)}, bf16[160,2560]{1,0:T(8,128)(2,1)S(1)}, u32[]{:S(2)}) copy-start(bf16[160,2560]{1,0:T(8,128)(2,1)S(1)} %fusion.22) | copy-start | bytes 2457604
  305.9 18.0 %collective-permute-start.3 = (bf16[160,2560]{1,0:T(8,128)(2,1)S(1)}, bf16[160,2560]{1,0:T(8,128)(2,1)S(1)}, u32[]{:S(2)}, u32[]{:S(2)}) collective-permute-start(bf16[160,2560]{1,0:T(8,128)(2,1)S(1)} %fusion.22), channel_id=1, source_target_pairs={{0,64},{16,80},{32,96},{48,112},{64,0},{80,16},{96,32},{112,48},{1... | collective-permute-start | bytes 2457608 | tf_op jit(solution)/shard_map/ppermute | solution.py:10
  325.4 32.5 %slice-start = ((s8[13107200]{0:T(1024)(128)(4,1)}), s8[524288]{0:T(1024)(128)(4,1)S(1)}, s32[]{:S(2)}) async-start(s8[13107200]{0:T(1024)(128)(4,1)} %bitcast.87), calls=%async_computation.11 | async-start | bytes 1048576
  327.4 30.5 %slice-start.1 = ((s8[13107200]{0:T(1024)(128)(4,1)}), s8[4194304]{0:T(1024)(128)(4,1)S(1)}, s32[]{:S(2)}) async-start(s8[13107200]{0:T(1024)(128)(4,1)} %bitcast.87), calls=%async_computation.12 | async-start | bytes 8388608
  381.9 15.3 %collective-permute-start.4 = (bf16[160,2560]{1,0:T(8,128)(2,1)}, bf16[160,2560]{1,0:T(8,128)(2,1)S(1)}, u32[]{:S(2)}, u32[]{:S(2)}) collective-permute-start(bf16[160,2560]{1,0:T(8,128)(2,1)} %gather_fusion.4), channel_id=1, source_target_pairs={{0,64},{16,80},{32,96},{48,112},{64,0},{80,16},{96,32},{112,48},{1... | collective-permute-start | bytes 2457608 | tf_op jit(solution)/shard_map/ppermute | solution.py:10
  405.9 26.9 %copy-start.5 = (bf16[160,2560]{1,0:T(8,128)(2,1)}, bf16[160,2560]{1,0:T(8,128)(2,1)S(1)}, u32[]{:S(2)}) copy-start(bf16[160,2560]{1,0:T(8,128)(2,1)S(1)} %add_convert_fusion.2) | copy-start | bytes 2457604
  434.5 13.9 %copy-start.6 = (bf16[160,2560]{1,0:T(8,128)(2,1)}, bf16[160,2560]{1,0:T(8,128)(2,1)S(1)}, u32[]{:S(2)}) copy-start(bf16[160,2560]{1,0:T(8,128)(2,1)S(1)} %fusion.23) | copy-start | bytes 2457604
  434.5 13.9 %collective-permute-start.5 = (bf16[160,2560]{1,0:T(8,128)(2,1)S(1)}, bf16[160,2560]{1,0:T(8,128)(2,1)S(1)}, u32[]{:S(2)}, u32[]{:S(2)}) collective-permute-start(bf16[160,2560]{1,0:T(8,128)(2,1)S(1)} %fusion.23), channel_id=1, source_target_pairs={{0,64},{16,80},{32,96},{48,112},{64,0},{80,16},{96,32},{112,48},{1... | collective-permute-start | bytes 2457608 | tf_op jit(solution)/shard_map/ppermute | solution.py:10
  449.9 30.2 %slice-start.4 = ((s8[13107200]{0:T(1024)(128)(4,1)}), s8[524288]{0:T(1024)(128)(4,1)S(1)}, s32[]{:S(2)}) async-start(s8[13107200]{0:T(1024)(128)(4,1)} %bitcast.89), calls=%async_computation.15 | async-start | bytes 1048576
  451.9 28.2 %slice-start.5 = ((s8[13107200]{0:T(1024)(128)(4,1)}), s8[4194304]{0:T(1024)(128)(4,1)S(1)}, s32[]{:S(2)}) async-start(s8[13107200]{0:T(1024)(128)(4,1)} %bitcast.89), calls=%async_computation.16 | async-start | bytes 8388608
  471.9 8.3 %slice-start.6 = ((s8[13107200]{0:T(1024)(128)(4,1)}), s8[4194304]{0:T(1024)(128)(4,1)S(1)}, s32[]{:S(2)}) async-start(s8[13107200]{0:T(1024)(128)(4,1)} %bitcast.89), calls=%async_computation.17 | async-start | bytes 8388608
  503.9 14.1 %collective-permute-start.6 = (bf16[160,2560]{1,0:T(8,128)(2,1)}, bf16[160,2560]{1,0:T(8,128)(2,1)S(1)}, u32[]{:S(2)}, u32[]{:S(2)}) collective-permute-start(bf16[160,2560]{1,0:T(8,128)(2,1)} %gather_fusion.6), channel_id=1, source_target_pairs={{0,64},{16,80},{32,96},{48,112},{64,0},{80,16},{96,32},{112,48},{1... | collective-permute-start | bytes 2457608 | tf_op jit(solution)/shard_map/ppermute | solution.py:10
  (7 other events, 38.7 us)
Sparse Core Ops, SparseCore 0:
  10.2 109.0 all-gather.2
  121.5 92.1 all-gather.4
where the time goes:
time: 574 us; the launch traced here: 565 us
  waiting for transfers between devices  234 us (41%)
  blocking collectives  131 us (23%)
  local copies, waits for them, and re-layouts  66.3 us (12%)
  matrix products  64.5 us (11%)
  starting transfers between devices  35.7 us (6%)
  other arithmetic  18.8 us (3%)
  between operations  15.1 us (3%)
    ppermute x7, waiting for transfers between devices, swapped(): lax.ppermute(value, axis, [(i, i ^ 1 << apart) for i in range(lax.axis_si...  98.4 us
    all_gather x1, waiting for transfers between devices, on_device(): lax.all_gather(partner_share, 'row', axis=0, tiled=True)  86.6 us
    all_to_all x3, blocking collectives, on_device(): lax.all_to_all(combined, 'row', split_axis=1, concat_axis=0, tiled=True)  57.8 us
    all_to_all x2, blocking collectives, on_device(): lax.all_to_all(outgoing, 'row', split_axis=1, concat_axis=1, tiled=True)  37.3 us
    all_to_all x2, blocking collectives, on_device(): lax.all_to_all(ph_prod.reshape(fanout, shard_count, state_count), 'row',...  35.9 us
    dot_general x3, matrix products, on_device(): jnp.dot(masked, full_own, preferred_element_type=jnp.float32)  26.7 us
    dot_general x3, matrix products, on_device(): near_part = jnp.dot(weighted, full_own, preferred_element_type=jnp.float32)  24.3 us
    all_gather x1, waiting for transfers between devices, on_device(): lax.all_gather(own_share, 'row', axis=0, tiled=True)  22.3 us
  transfers between devices with their start and end apart: 11, of which 11 were waited for; matrix products, arithmetic and copies ran while one was open for 7% of the time, Pallas kernels for 0%

commit v1 on v0

v1 whole, which is shorter than its diff:
```python
import jax
import jax.numpy as jnp
from jax import lax
from jax.sharding import Mesh, PartitionSpec as P

TERMS = 3


def swapped(value):
    return lax.ppermute(value, "hi", [(0, 1), (1, 0)])


def on_device(
    generator, hamiltonian, live_states, pp_occupation, ph_occupation, ph_order, recoupling
):
    row_count = generator.shape[1]
    state_count = generator.shape[2]
    half = row_count // 2
    shard_count = lax.axis_size("row")
    hi = lax.axis_index("hi")
    lo = lax.axis_index("lo")
    my_shard = lax.axis_index("row")
    first = hi == 0
    r0 = recoupling[lo]
    r1 = recoupling[lo + lax.axis_size("lo")]
    positions = jnp.arange(state_count, dtype=jnp.int32)
    live_count = live_states[0]
    column_alive = positions < live_count
    row_alive = my_shard * row_count + jnp.arange(row_count, dtype=jnp.int32) < live_count
    block_alive = row_alive[:, None] & column_alive[None, :]
    own_share = jnp.where(block_alive, generator[0], jnp.zeros_like(generator[0]))
    far_share = swapped(own_share)
    full_own = lax.all_gather(own_share, "row", axis=0, tiled=True)
    full_far = lax.all_gather(far_share, "row", axis=0, tiled=True)

    pp = jnp.where(column_alive, pp_occupation[0], 0)
    ph = jnp.zeros((state_count,), jnp.int32).at[ph_order[0]].set(ph_occupation[0])
    ph = jnp.where(column_alive, ph, 0)
    mine = jnp.stack([pp, ph]).astype(jnp.float32)
    other = swapped(mine)
    d0, n0 = jnp.where(first, mine, other)
    d1, n1 = jnp.where(first, other, mine)
    a0 = d0 + r0[0] ** 3 * n0 + r1[1] ** 3 * n1
    a1 = d1 + r1[0] ** 3 * n1 + r0[1] ** 3 * n0
    p = r0[0] ** 2 * r0[1] * n0 + r1[1] ** 2 * r1[0] * n1
    q = r1[0] ** 2 * r1[1] * n1 + r0[1] ** 2 * r0[0] * n0
    zero_set = jnp.stack([a0, p, p, q])
    one_set = jnp.stack([p, q, q, a1])
    own_set = jnp.where(first, zero_set, one_set)
    far_set = jnp.where(first, one_set, zero_set)

    own_ham = jnp.where(block_alive, hamiltonian[0], jnp.zeros_like(hamiltonian[0]))
    keep = lax.dynamic_slice_in_dim(own_ham, hi * half, half, 0)
    gone = lax.dynamic_slice_in_dim(own_ham, (1 - hi) * half, half, 0)
    came = swapped(gone)
    current = jnp.concatenate([jnp.where(first, keep, came), jnp.where(first, came, keep)])
    running = jnp.zeros(current.shape, jnp.float32)

    def mix(x, s):
        x0, x1 = x[:half], x[half:]
        top = x0 * s[0] + x1 * s[1]
        low = x0 * s[2] + x1 * s[3]
        return jnp.concatenate([top, low]).astype(jnp.bfloat16)

    for term_index in range(1, TERMS + 1):
        wide = current.astype(jnp.float32)
        combined = jnp.dot(
            mix(wide, own_set), full_own, preferred_element_type=jnp.float32
        ) + jnp.dot(mix(wide, far_set), full_far, preferred_element_type=jnp.float32)
        combined = combined.astype(jnp.bfloat16)
        if term_index < TERMS:
            sent = combined.T
            got = lax.all_to_all(sent, ("row", "hi"), split_axis=0, concat_axis=0, tiled=True)
            got = got.reshape(2 * shard_count, half, 2, half)
            flipped = jnp.transpose(got, (2, 1, 0, 3)).reshape(row_count, state_count)
            increment = -(combined.astype(jnp.float32) + flipped.astype(jnp.float32)) / term_index
            running = running + increment
            current = increment.astype(jnp.bfloat16)
    running = running - combined.astype(jnp.float32) / TERMS
    leaving = lax.dynamic_slice_in_dim(running, (1 - hi) * half, half, 0).astype(jnp.bfloat16)
    staying = lax.dynamic_slice_in_dim(running, hi * half, half, 0)
    landed = swapped(leaving).astype(jnp.float32)
    blocks = combined.reshape(2, half, shard_count, row_count)
    blocks = jnp.transpose(blocks, (0, 2, 3, 1)).reshape(2 * state_count, half)
    got = lax.all_to_all(blocks, ("hi", "row"), split_axis=0, concat_axis=0, tiled=True)
    got = got.reshape(2, shard_count, row_count, half)
    flipped = jnp.transpose(got, (2, 1, 0, 3)).reshape(row_count, state_count)
    rows = jnp.concatenate(
        [jnp.where(first, staying, landed), jnp.where(first, landed, staying)]
    )
    return (own_ham.astype(jnp.float32) + rows - flipped.astype(jnp.float32) / TERMS)[None]


def solution(mesh):
    chans, rows = mesh.devices.shape
    pairs = Mesh(mesh.devices.reshape(2, chans // 2, rows), ("hi", "lo", "row"))
    chan = ("hi", "lo")
    placed = (
        P(chan, "row", None),
        P(chan, "row", None),
        P(chan),
        P(chan, None),
        P(chan, None),
        P(chan, None),
        P(),
    )
    return jax.shard_map(
        on_device, mesh=pairs, in_specs=placed, out_specs=P(chan, "row", None), check_vma=False
    )
```

time: 574 us -> 353 us (0.61); the launches traced: 565 us -> 353 us
  blocking collectives: 131 us -> 54 us
  waiting for transfers between devices: 234 us -> 167 us
  matrix products: 64.5 us -> 36 us
  local copies, waits for them, and re-layouts: 66.3 us -> 43.7 us
  starting transfers between devices: 35.7 us -> 13.6 us
  between operations: 15.1 us -> 24.5 us
    ppermute x7 -> x4, waiting for transfers between devices: 98.4 us -> 18.8 us  [swapped(): return lax.ppermute(value, 'hi', [(0, 1), (1, 0)])]
    all_to_all x7 -> x2, blocking collectives: 131 us -> 54 us  [on_device(): lax.all_to_all(sent, ('row', 'hi'), split_axis=0, concat_axis=0, tiled=True)]
    dot_general x9 -> x6, matrix products: 64.5 us -> 36 us  [the longest x3 22.7 us: on_device(): jnp.dot(mix(wide, own_set), full_own, preferred_element_type=jnp.float32)]
    all_gather x2, waiting for transfers between devices: 109 us -> 133 us  [the longest x1 86.2 us: on_device(): full_far = lax.all_gather(far_share, 'row', axis=0, tiled=True)]
    gather x7 -> x0, local copies, waits for them, and re-layouts: 23.8 us -> none  [the longest x1 13.6 us: on_device(): ph_occupation[0][inverse]]
    ppermute x7 -> x4, starting transfers between devices: 22.2 us -> 7.6 us  [swapped(): return lax.ppermute(value, 'hi', [(0, 1), (1, 0)])]
    all_to_all x2 -> x1, waiting for transfers between devices: 26.3 us -> 14.9 us  [on_device(): lax.all_to_all(blocks, ('hi', 'row'), split_axis=0, concat_axis=0, tiled=...]
    all_to_all x2 -> x1, starting transfers between devices: 13.5 us -> 5.96 us  [on_device(): lax.all_to_all(blocks, ('hi', 'row'), split_axis=0, concat_axis=0, tiled=...]
  transfers between devices with their start and end apart: 11 -> 7, of which waited for: 11 -> 5; matrix products, arithmetic and copies ran while one was open for 7% -> 8% of each run, Pallas kernels for 0% -> 0%
where the time goes in v1:
time: 353 us
  waiting for transfers between devices  167 us (47%)
  blocking collectives  54 us (15%)
  local copies, waits for them, and re-layouts  43.7 us (12%)
  matrix products  36 us (10%)
  between operations  24.5 us (7%)
  other arithmetic  14.2 us (4%)
  starting transfers between devices  13.6 us (4%)
    all_gather x1, waiting for transfers between devices, on_device(): full_far = lax.all_gather(far_share, 'row', axis=0, tiled=True)  86.2 us
    all_to_all x2, blocking collectives, on_device(): lax.all_to_all(sent, ('row', 'hi'), split_axis=0, concat_axis=0, tiled=True)  54 us
    all_gather x1, waiting for transfers between devices, on_device(): full_own = lax.all_gather(own_share, 'row', axis=0, tiled=True)  46.6 us
    dot_general x3, matrix products, on_device(): jnp.dot(mix(wide, own_set), full_own, preferred_element_type=jnp.float32)  22.7 us
    ppermute x4, waiting for transfers between devices, swapped(): return lax.ppermute(value, 'hi', [(0, 1), (1, 0)])  18.8 us
    all_to_all x1, waiting for transfers between devices, on_device(): lax.all_to_all(blocks, ('hi', 'row'), split_axis=0, concat_axis=0, tiled=...  14.9 us
    dot_general x3, matrix products, on_device(): jnp.dot(mix(wide, far_set), full_far, preferred_element_type=jnp.float32)  13.3 us
    convert_element_type x4, local copies, waits for them, and re-layouts, on_device(): flipped.astype(jnp.float32)  12.8 us
  transfers between devices with their start and end apart: 7, of which 5 were waited for; matrix products, arithmetic and copies ran while one was open for 8% of the time, Pallas kernels for 0%

profile of v1, /device:TPU:0, one launch (start us, length us, event | category | flops | bytes accessed | tf_op | source)
XLA Modules:
  0.0 352.6 jit_solution(11028163509748805113)
XLA Ops:
  7.2 2.8 and_select_fusion.1
  10.1 3.2 collective-permute-start.2
  13.3 18.5 %collective-permute-done.2 = bf16[160,2560]{1,0:T(8,128)(2,1)S(1)} collective-permute-done((bf16[160,2560]{1,0:T(8,128)(2,1)}, bf16[160,2560]{1,0:T(8,128)(2,1)S(1)}, u32[]{:S(2)}, u32[]{:S(2)}) %collective-permute-start.2) | collective-permute-done | bytes 819232 | tf_op jit(solution)/shard_map/ppermute | solution.py:10
  32.7 9.9 %scatter_custom_fusion = s32[2560]{0:T(1024)S(1)} fusion(s32[2560]{0:T(1024)S(1)} %fusion.31, s32[2560]{0:T(1024)S(1)} %reduce.1, s32[]{:T(128)} %constant.13.clone.1), kind=kCustom, calls=%fused_computation.88 | custom fusion | bytes 10244 | tf_op jit(solution)/shard_map/scatter | solution.py:37
  42.8 3.3 collective-permute-start.1
  58.6 46.6 %all-gather.3.cloned.1.call-done = bf16[2560,2560]{1,0:T(8,128)(2,1)} async-done(((bf16[160,2560]{1,0:T(8,128)(2,1)}), bf16[2560,2560]{1,0:T(8,128)(2,1)}) %all-gather.3.cloned.1.call-update) | async-done | bytes 13107216 | tf_op jit(solution)/shard_map/all_gather | solution.py:33
  105.2 8.2 %fusion.10 = f32[160,2560]{1,0:T(8,128)} fusion(bf16[2560,2560]{1,0:T(8,128)(2,1)} %all-gather.3.cloned.1.call-done, bf16[80,2560]{1,0:T(8,128)(2,1)S(1)} %get-tuple-element.26, bf16[80,2560]{1,0:T(8,128)(2,1)S(1)} %get-tuple-element.25), kind=kOutput, calls=%fused_computation.26 | convolution fusion | flops 2098790400 | bytes 15564800 | tf_op jit(solution)/shard_map/dot_general | solution.py:67
  113.4 86.2 %all-gather.5.cloned.1.call-done = bf16[2560,2560]{1,0:T(8,128)(2,1)} async-done(((bf16[160,2560]{1,0:T(8,128)(2,1)}), bf16[2560,2560]{1,0:T(8,128)(2,1)}) %all-gather.5.cloned.1.call-update) | async-done | bytes 13107216 | tf_op jit(solution)/shard_map/all_gather | solution.py:34
  199.6 7.5 %fusion = bf16[160,2560]{1,0:T(8,128)(2,1)S(1)} fusion(f32[160,2560]{1,0:T(8,128)} %fusion.10, bf16[2560,2560]{1,0:T(8,128)(2,1)} %all-gather.5.cloned.1.call-done, bf16[80,2560]{1,0:T(8,128)(2,1)S(1)} %get-tuple-element.24, bf16[80,2560]{1,0:T(8,128)(2,1)S(1)} %get-tuple-element.23), kind=kOutput, calls=%fused_computation.4 | convolution fusion | flops 2099609600 | bytes 16384000 | tf_op jit(solution)/shard_map/dot_general | solution.py:69
  209.3 29.8 %all_to_all.27 = bf16[32,80,160]{1,2,0:T(8,128)(2,1)S(1)} all-to-all(bf16[32,80,160]{1,2,0:T(8,128)(2,1)S(1)} %copy.14), channel_id=1, replica_groups=mesh['hi'=2,'lo'=4,'row'=16] {'row','hi'}, dimensions={0} | all-to-all | bytes 1638400 | tf_op jit(solution)/shard_map/all_to_all | solution.py:73
  239.1 2.7 copy.15
  241.7 2.9 reshape.143
  245.3 7.3 %fusion.17 = f32[160,2560]{1,0:T(8,128)S(1)} fusion(bf16[2560,2560]{1,0:T(8,128)(2,1)} %all-gather.3.cloned.1.call-done, bf16[80,2560]{1,0:T(8,128)(2,1)S(1)} %get-tuple-element.22, bf16[80,2560]{1,0:T(8,128)(2,1)S(1)} %get-tuple-element.21), kind=kOutput, calls=%fused_computation.33 | convolution fusion | flops 2098790400 | bytes 15564800 | tf_op jit(solution)/shard_map/dot_general | solution.py:67
  255.5 2.4 all_to_all.20
  259.8 24.2 %all_to_all.28 = bf16[32,80,160]{1,2,0:T(8,128)(2,1)S(1)} all-to-all(bf16[32,80,160]{1,2,0:T(8,128)(2,1)S(1)} %copy.16), channel_id=1, replica_groups=mesh['hi'=2,'lo'=4,'row'=16] {'row','hi'}, dimensions={0} | all-to-all | bytes 1638400 | tf_op jit(solution)/shard_map/all_to_all | solution.py:73
  285.8 4.3 %copy.17 = f32[2,80,32,80]{3,2,1,0:T(8,128)} copy(f32[2,80,32,80]{1,3,0,2:T(8,128)} %convert_bitcast_fusion) | data formatting | bytes 3276800 | tf_op jit(solution)/shard_map/convert_element_type | solution.py:76
  290.1 2.9 reshape.144
  295.0 7.2 %fusion.24 = f32[160,2560]{1,0:T(8,128)S(1)} fusion(bf16[2560,2560]{1,0:T(8,128)(2,1)} %all-gather.3.cloned.1.call-done, bf16[80,2560]{1,0:T(8,128)(2,1)S(1)} %get-tuple-element.18, bf16[80,2560]{1,0:T(8,128)(2,1)S(1)} %get-tuple-element.17), kind=kOutput, calls=%fused_computation.40 | convolution fusion | flops 2098790400 | bytes 15564800 | tf_op jit(solution)/shard_map/dot_general | solution.py:67
  302.4 3.5 multiply_subtract_fusion
  307.0 2.6 reshape.142
  311.9 6.0 %all-to-all-start.2 = ((bf16[32,160,80]{2,1,0:T(8,128)(2,1)}), bf16[32,160,80]{2,1,0:T(8,128)(2,1)S(1)}, u32[]{:S(2)}, u32[]{:S(2)}) async-start(bf16[32,160,80]{2,1,0:T(8,128)(2,1)} %bitcast.17), calls=%async_computation.2 | async-start | bytes 2621440 | tf_op jit(solution)/shard_map/all_to_all | solution.py:85
  320.3 14.9 %all-to-all-done.2 = bf16[32,160,80]{2,1,0:T(8,128)(2,1)S(1)} async-done(((bf16[32,160,80]{2,1,0:T(8,128)(2,1)}), bf16[32,160,80]{2,1,0:T(8,128)(2,1)S(1)}, u32[]{:S(2)}, u32[]{:S(2)}) %all-to-all-start.2) | async-done | bytes 819232 | tf_op jit(solution)/shard_map/all_to_all | solution.py:85
  337.6 4.7 %div.26 = f32[1,160,2560]{2,1,0:T(8,128)} reshape(f32[160,16,2,80]{3,2,1,0:T(2,128)S(1)} %copy.19) | data formatting | bytes 3276800 | tf_op jit(solution)/shard_map/div | solution.py:91
  342.3 3.5 fusion.3
  (84 shorter events, 22.9 us)
Async XLA Ops:
  6.5 98.7 %all-gather.3.cloned.1.call-start = ((), (), s32[]{:S(2)}) async-start(), calls=%async_computation.3 | async-start | bytes 13926400 | tf_op jit(solution)/shard_map/all_gather | solution.py:33
  10.0 22.7 %copy-start.8 = (s32[1,2560]{1,0:T(1,128)S(1)}, s32[1,2560]{1,0:T(1,128)}, u32[]{:S(2)}) copy-start(s32[1,2560]{1,0:T(1,128)} %param.11) | copy-start | bytes 30724
  10.0 22.7 %copy-start.9 = (s32[1,2560]{1,0:T(1,128)S(1)}, s32[1,2560]{1,0:T(1,128)}, u32[]{:S(2)}) copy-start(s32[1,2560]{1,0:T(1,128)} %param.12) | copy-start | bytes 30724
  10.0 32.7 %copy-start.10 = (s32[1,2560]{1,0:T(1,128)S(1)}, s32[1,2560]{1,0:T(1,128)}, u32[]{:S(2)}) copy-start(s32[1,2560]{1,0:T(1,128)} %param.10) | copy-start | bytes 30724
  10.0 36.5 %copy-start.11 = (f32[8,2]{0,1:T(2,128)S(1)}, f32[8,2]{0,1:T(2,128)}, u32[]{:S(2)}) copy-start(f32[8,2]{0,1:T(2,128)} %param.13) | copy-start | bytes 196
  10.0 189.6 %all-gather.5.cloned.1.call-start = ((), (), s32[]{:S(2)}) async-start(), calls=%async_computation.4 | async-start | bytes 13926400 | tf_op jit(solution)/shard_map/all_gather | solution.py:34
  10.1 21.7 %collective-permute-start.2 = (bf16[160,2560]{1,0:T(8,128)(2,1)}, bf16[160,2560]{1,0:T(8,128)(2,1)S(1)}, u32[]{:S(2)}, u32[]{:S(2)}) collective-permute-start(bf16[160,2560]{1,0:T(8,128)(2,1)} %get-tuple-element.38), channel_id=1, source_target_pairs={{0,64},{64,0},{1,65},{65,1},{2,66},{66,2},{3,67},{67,3},{4,68},{68... | collective-permute-start | bytes 2457608 | tf_op jit(solution)/shard_map/ppermute | solution.py:10
  42.8 14.3 %collective-permute-start.1 = (f32[2,2560]{1,0:T(2,128)S(1)}, f32[2,2560]{1,0:T(2,128)S(1)}, u32[]{:S(2)}, u32[]{:S(2)}) collective-permute-start(f32[2,2560]{1,0:T(2,128)S(1)} %add_convert_fusion.12), channel_id=1, source_target_pairs={{0,64},{64,0},{1,65},{65,1},{2,66},{66,2},{3,67},{67,3},{4,68},{68... | collective-permute-start | bytes 61448 | tf_op jit(solution)/shard_map/ppermute | solution.py:10
  46.1 11.8 %collective-permute-start = (bf16[80,2560]{1,0:T(8,128)(2,1)S(1)}, bf16[80,2560]{1,0:T(8,128)(2,1)S(1)}, u32[]{:S(2)}, u32[]{:S(2)}) collective-permute-start(bf16[80,2560]{1,0:T(8,128)(2,1)S(1)} %constant_dynamic-slice_fusion.2), channel_id=1, source_target_pairs={{0,64},{64,0},{1,65},{65,1},{2,66},{66,2},{3,67},{67,3},{4,68},{68... | collective-permute-start | bytes 1228808 | tf_op jit(solution)/shard_map/ppermute | solution.py:10
  207.1 37.5 %copy-start = (bf16[160,2560]{1,0:T(8,128)(2,1)}, bf16[160,2560]{1,0:T(8,128)(2,1)S(1)}, u32[]{:S(2)}) copy-start(bf16[160,2560]{1,0:T(8,128)(2,1)S(1)} %fusion) | copy-start | bytes 2457604
  244.7 8.0 %slice-start = ((s8[13107200]{0:T(1024)(128)(4,1)}), s8[4194304]{0:T(1024)(128)(4,1)S(1)}, s32[]{:S(2)}) async-start(s8[13107200]{0:T(1024)(128)(4,1)} %bitcast.49), calls=%async_computation.5 | async-start | bytes 8388608
  244.9 7.8 %slice-start.1 = ((s8[13107200]{0:T(1024)(128)(4,1)}), s8[4194304]{0:T(1024)(128)(4,1)S(1)}, s32[]{:S(2)}) async-start(s8[13107200]{0:T(1024)(128)(4,1)} %bitcast.49), calls=%async_computation.6 | async-start | bytes 8388608
  245.3 7.9 %slice-start.2 = ((s8[13107200]{0:T(1024)(128)(4,1)}), s8[4194304]{0:T(1024)(128)(4,1)S(1)}, s32[]{:S(2)}) async-start(s8[13107200]{0:T(1024)(128)(4,1)} %bitcast.49), calls=%async_computation.7 | async-start | bytes 8388608
  245.3 7.9 %slice-start.3 = ((s8[13107200]{0:T(1024)(128)(4,1)}), s8[524288]{0:T(1024)(128)(4,1)S(1)}, s32[]{:S(2)}) async-start(s8[13107200]{0:T(1024)(128)(4,1)} %bitcast.49), calls=%async_computation.8 | async-start | bytes 1048576
  293.0 9.2 %slice-start.4 = ((s8[13107200]{0:T(1024)(128)(4,1)}), s8[4194304]{0:T(1024)(128)(4,1)S(1)}, s32[]{:S(2)}) async-start(s8[13107200]{0:T(1024)(128)(4,1)} %bitcast.51), calls=%async_computation.9 | async-start | bytes 8388608
  294.6 7.7 %slice-start.5 = ((s8[13107200]{0:T(1024)(128)(4,1)}), s8[4194304]{0:T(1024)(128)(4,1)S(1)}, s32[]{:S(2)}) async-start(s8[13107200]{0:T(1024)(128)(4,1)} %bitcast.51), calls=%async_computation.10 | async-start | bytes 8388608
  295.0 7.3 %slice-start.6 = ((s8[13107200]{0:T(1024)(128)(4,1)}), s8[4194304]{0:T(1024)(128)(4,1)S(1)}, s32[]{:S(2)}) async-start(s8[13107200]{0:T(1024)(128)(4,1)} %bitcast.51), calls=%async_computation.11 | async-start | bytes 8388608
  295.0 7.3 %slice-start.7 = ((s8[13107200]{0:T(1024)(128)(4,1)}), s8[524288]{0:T(1024)(128)(4,1)S(1)}, s32[]{:S(2)}) async-start(s8[13107200]{0:T(1024)(128)(4,1)} %bitcast.51), calls=%async_computation.12 | async-start | bytes 1048576
  295.0 7.3 %copy-start.1 = (bf16[160,2560]{1,0:T(8,128)(2,1)S(1)}, bf16[160,2560]{1,0:T(8,128)(2,1)}, u32[]{:S(2)}) copy-start(bf16[160,2560]{1,0:T(8,128)(2,1)} %copy-done) | copy-start | bytes 2457604
  295.0 7.4 %copy-start.3 = (bf16[160,2560]{1,0:T(8,128)(2,1)S(1)}, bf16[160,2560]{1,0:T(8,128)(2,1)}, u32[]{:S(2)}) copy-start(bf16[160,2560]{1,0:T(8,128)(2,1)} %copy-done.2) | copy-start | bytes 2457604
  305.9 12.0 %collective-permute-start.3 = (bf16[80,2560]{1,0:T(8,128)(2,1)S(1)}, bf16[80,2560]{1,0:T(8,128)(2,1)}, u32[]{:S(2)}, u32[]{:S(2)}) collective-permute-start(bf16[80,2560]{1,0:T(8,128)(2,1)S(1)} %dynamic-slice_convert_fusion), channel_id=1, source_target_pairs={{0,64},{64,0},{1,65},{65,1},{2,66},{66,2},{3,67},{67,3},{4,68},{68... | collective-permute-start | bytes 1228808 | tf_op jit(solution)/shard_map/ppermute | solution.py:10
  311.9 6.0 %copy-start.5 = (f32[160,2560]{1,0:T(8,128)S(1)}, f32[160,2560]{1,0:T(8,128)}, u32[]{:S(2)}) copy-start(f32[160,2560]{1,0:T(8,128)} %copy-done.4) | copy-start | bytes 4915204
  311.9 23.3 %all-to-all-start.2 = ((bf16[32,160,80]{2,1,0:T(8,128)(2,1)}), bf16[32,160,80]{2,1,0:T(8,128)(2,1)S(1)}, u32[]{:S(2)}, u32[]{:S(2)}) async-start(bf16[32,160,80]{2,1,0:T(8,128)(2,1)} %bitcast.17), calls=%async_computation.2 | async-start | bytes 2621440 | tf_op jit(solution)/shard_map/all_to_all | solution.py:85
  337.6 4.7 %copy-start.6 = (bf16[1,160,2560]{2,1,0:T(8,128)(2,1)S(1)}, bf16[1,160,2560]{2,1,0:T(8,128)(2,1)}, u32[]{:S(2)}) copy-start(bf16[1,160,2560]{2,1,0:T(8,128)(2,1)} %param.8) | copy-start | bytes 2457604
  (3 other events, 6.3 us)
Sparse Core Ops, SparseCore 0:
  10.1 95.0 all-gather.2
  107.4 92.1 all-gather.4

commit v2 on v1

v2 whole, which is shorter than its diff:
```python
import functools

import jax
import jax.numpy as jnp
from jax import lax
from jax.experimental import pallas as pl
from jax.experimental.pallas import tpu as pltpu
from jax.sharding import Mesh, PartitionSpec as P

TERMS = 3
LANES = 128
STEP = 32
BF = jnp.bfloat16
F32 = jnp.float32
VMEM = pl.BlockSpec(memory_space=pltpu.VMEM)
SMEM = pl.BlockSpec(memory_space=pltpu.SMEM)


def tile_at(index):
    return pl.ds(pl.multiple_of(index * LANES, LANES), LANES)


def pack_kernel(sent_tiles, tiles, scalars, gen_ref, out_ref):
    start, live = scalars[0], scalars[1]
    for group in range(gen_ref.shape[0] // STEP):
        rows = pl.ds(group * STEP, STEP)
        first_row = start + group * STEP
        diagonal = first_row // LANES
        row_at = first_row + lax.broadcasted_iota(jnp.int32, (STEP, LANES), 0)
        for apart in range(sent_tiles):
            tile = lax.rem(diagonal + apart, tiles)
            column_at = tile * LANES + lax.broadcasted_iota(jnp.int32, (STEP, LANES), 1)
            alive = (row_at < live) & (column_at < live)
            value = gen_ref[rows, tile_at(tile)].astype(F32)
            out_ref[rows, apart * LANES : (apart + 1) * LANES] = jnp.where(
                alive, value, 0.0
            ).astype(BF)


def unpack_kernel(blocks, sent_tiles, tiles, got_ref, out_ref, held, sems):
    matrix, a = pl.program_id(0), pl.program_id(1)
    rows = got_ref.shape[2]

    def copies(which):
        return [
            pltpu.make_async_copy(
                got_ref.at[block, which],
                held.at[which, pl.ds(block * rows, rows)],
                sems.at[which, block],
            )
            for block in range(blocks)
        ]

    @pl.when((matrix == 0) & (a == 0))
    def _():
        for which in range(2):
            for copy in copies(which):
                copy.start()

    for which in range(2):

        @pl.when((matrix == which) & (a == 0))
        def _(which=which):
            for copy in copies(which):
                copy.wait()

    for apart in range(tiles):
        b = lax.rem(a + apart, tiles)
        if apart < sent_tiles:
            value = held[matrix, tile_at(a), apart * LANES : (apart + 1) * LANES]
        else:
            back = tiles - apart
            value = held[matrix, tile_at(b), back * LANES : (back + 1) * LANES]
            value = (-value).T
        out_ref[0, :, tile_at(b)] = value


def send_kernel(half, c_ref, out_ref):
    filler = jnp.zeros((LANES - half, LANES), F32)
    for tile in range(c_ref.shape[1] // LANES):
        at = slice(tile * LANES, (tile + 1) * LANES)
        for channel in range(2):
            block = c_ref[channel * half : (channel + 1) * half, at].astype(F32)
            block = jnp.concatenate([block, filler]).T
            out_ref[at, channel * LANES : (channel + 1) * LANES] = block.astype(BF)


def laid_out(pieces, half, tile):
    lane = lax.broadcasted_iota(jnp.int32, (1, LANES), 1)
    low = tile * LANES
    result = None
    for piece in range(low // half, (low + LANES - 1) // half + 1):
        shift = (piece * half - low) % LANES
        value = pieces(piece)
        if shift:
            value = pltpu.roll(value, shift, 1)
        begin = piece * half - low
        inside = lane >= begin
        result = value if result is None else jnp.where(inside, value, result)
    return result


def mix(x0, x1, weights, out_ref, half, at):
    out_ref[:half, at] = (x0 * weights[0:1] + x1 * weights[1:2]).astype(BF)
    out_ref[half:, at] = (x0 * weights[2:3] + x1 * weights[3:4]).astype(BF)


def start_kernel(half, x_ref, own_ref, far_ref, a_own, a_far):
    for tile in range(x_ref.shape[1] // LANES):
        at = slice(tile * LANES, (tile + 1) * LANES)
        x0, x1 = x_ref[:half, at].astype(F32), x_ref[half:, at].astype(F32)
        mix(x0, x1, own_ref[:, at], a_own, half, at)
        mix(x0, x1, far_ref[:, at], a_far, half, at)


def update_kernel(half, scale, c_ref, got_ref, run_ref, own_ref, far_ref, run_out, a_own, a_far):
    for tile in range(c_ref.shape[1] // LANES):
        at = slice(tile * LANES, (tile + 1) * LANES)
        xs = []
        for channel in range(2):
            lanes = slice(channel * LANES, (channel + 1) * LANES)
            flipped = laid_out(lambda s: got_ref[s, :, lanes].astype(F32), half, tile)
            rows = slice(channel * half, (channel + 1) * half)
            increment = (c_ref[rows, at].astype(F32) + flipped) * scale
            run_out[rows, at] = run_ref[rows, at] + increment
            xs.append(increment.astype(BF).astype(F32))
        mix(xs[0], xs[1], own_ref[:, at], a_own, half, at)
        mix(xs[0], xs[1], far_ref[:, at], a_far, half, at)


def end_kernel(half, scale, first_ref, ham_ref, stay_ref, land_ref, got_ref, out_ref):
    first = first_ref[0] != 0
    for tile in range(ham_ref.shape[1] // LANES):
        at = slice(tile * LANES, (tile + 1) * LANES)
        flipped = laid_out(
            lambda s: got_ref[s % 2, s // 2].astype(F32), half, tile
        )
        total = ham_ref[:, at].astype(F32) + flipped * scale
        stay, land = stay_ref[:, at], land_ref[:, at].astype(F32)
        out_ref[:half, at] = total[:half] + jnp.where(first, stay, land)
        out_ref[half:, at] = total[half:] + jnp.where(first, land, stay)


def call(kernel, out_shape, specs, name, megabytes=0):
    single = not isinstance(out_shape, (list, tuple))
    return pl.pallas_call(
        kernel,
        out_shape=out_shape,
        in_specs=specs,
        out_specs=VMEM if single else [VMEM] * len(out_shape),
        compiler_params=pltpu.CompilerParams(vmem_limit_bytes=24 << 20),
        name=name,
    )


def swapped(value):
    return lax.ppermute(value, "hi", [(0, 1), (1, 0)])


def on_device(
    generator, hamiltonian, live_states, pp_occupation, ph_occupation, ph_order, recoupling
):
    row_count = generator.shape[1]
    state_count = generator.shape[2]
    half = row_count // 2
    shard_count = lax.axis_size("row")
    tiles = state_count // LANES
    sent_tiles = tiles // 2 + 1
    hi = lax.axis_index("hi")
    lo = lax.axis_index("lo")
    my_shard = lax.axis_index("row")
    first = hi == 0
    shape = jax.ShapeDtypeStruct
    r0 = recoupling[lo]
    r1 = recoupling[lo + lax.axis_size("lo")]
    positions = jnp.arange(state_count, dtype=jnp.int32)
    live_count = live_states[0]
    column_alive = positions < live_count
    row_alive = my_shard * row_count + jnp.arange(row_count, dtype=jnp.int32) < live_count
    block_alive = row_alive[:, None] & column_alive[None, :]

    share = call(
        functools.partial(pack_kernel, sent_tiles, tiles),
        shape((row_count, sent_tiles * LANES), BF),
        [SMEM, VMEM],
        "pack",
    )(jnp.stack([my_shard * row_count, live_count]), generator[0])
    both = jnp.stack([share, swapped(share)])
    gathered = lax.all_gather(both, "row", axis=0, tiled=False)
    omegas = pl.pallas_call(
        functools.partial(unpack_kernel, shard_count, sent_tiles, tiles),
        grid=(2, tiles),
        out_shape=shape((2, state_count, state_count), BF),
        in_specs=[pl.BlockSpec(memory_space=pl.ANY)],
        out_specs=pl.BlockSpec((1, LANES, state_count), lambda m, a: (m, a, 0)),
        scratch_shapes=[
            pltpu.VMEM((2, state_count, sent_tiles * LANES), BF),
            pltpu.SemaphoreType.DMA((2, shard_count)),
        ],
        compiler_params=pltpu.CompilerParams(vmem_limit_bytes=24 << 20),
        name="unpack",
    )(gathered)

    pp = jnp.where(column_alive, pp_occupation[0], 0)
    ph = jnp.zeros((state_count,), jnp.int32).at[ph_order[0]].set(ph_occupation[0])
    ph = jnp.where(column_alive, ph, 0)
    mine = jnp.stack([pp, ph]).astype(F32)
    other = swapped(mine)
    d0, n0 = jnp.where(first, mine, other)
    d1, n1 = jnp.where(first, other, mine)
    a0 = d0 + r0[0] ** 3 * n0 + r1[1] ** 3 * n1
    a1 = d1 + r1[0] ** 3 * n1 + r0[1] ** 3 * n0
    p = r0[0] ** 2 * r0[1] * n0 + r1[1] ** 2 * r1[0] * n1
    q = r1[0] ** 2 * r1[1] * n1 + r0[1] ** 2 * r0[0] * n0
    zero_set = jnp.stack([a0, p, p, q])
    one_set = jnp.stack([p, q, q, a1])
    own_set = jnp.where(first, zero_set, one_set)
    far_set = jnp.where(first, one_set, zero_set)

    own_ham = jnp.where(block_alive, hamiltonian[0], jnp.zeros_like(hamiltonian[0]))
    keep = lax.dynamic_slice_in_dim(own_ham, hi * half, half, 0)
    gone = lax.dynamic_slice_in_dim(own_ham, (1 - hi) * half, half, 0)
    came = swapped(gone)
    current = jnp.concatenate([jnp.where(first, keep, came), jnp.where(first, came, keep)])
    running = jnp.zeros(current.shape, F32)
    mixed_shape = shape((row_count, state_count), BF)
    mixed_own, mixed_far = call(
        functools.partial(start_kernel, half), [mixed_shape] * 2, [VMEM] * 3, "start"
    )(current, own_set, far_set)

    for term_index in range(1, TERMS + 1):
        combined = jnp.dot(mixed_own, omegas[0], preferred_element_type=F32) + jnp.dot(
            mixed_far, omegas[1], preferred_element_type=F32
        )
        combined = combined.astype(BF)
        columns = call(
            functools.partial(send_kernel, half),
            shape((state_count, 2 * LANES), BF),
            [VMEM],
            "send",
        )(combined)
        if term_index < TERMS:
            got = lax.all_to_all(
                columns.reshape(2 * shard_count, half, 2 * LANES),
                ("row", "hi"),
                split_axis=0,
                concat_axis=0,
                tiled=True,
            )
            running, mixed_own, mixed_far = call(
                functools.partial(update_kernel, half, -1.0 / term_index),
                [shape((row_count, state_count), F32), mixed_shape, mixed_shape],
                [VMEM] * 5,
                "update",
            )(combined, got, running, own_set, far_set)
    running = running - combined.astype(F32) / TERMS
    leaving = lax.dynamic_slice_in_dim(running, (1 - hi) * half, half, 0).astype(BF)
    staying = lax.dynamic_slice_in_dim(running, hi * half, half, 0)
    landed = swapped(leaving)
    blocks = columns.reshape(shard_count, row_count, 2, LANES)
    blocks = jnp.transpose(blocks, (2, 0, 1, 3)).reshape(2 * shard_count, row_count, LANES)
    got = lax.all_to_all(blocks, ("hi", "row"), split_axis=0, concat_axis=0, tiled=True)
    result = call(
        functools.partial(end_kernel, half, -1.0 / TERMS),
        shape((row_count, state_count), F32),
        [SMEM] + [VMEM] * 4,
        "finish",
    )(
        first.astype(jnp.int32)[None],
        own_ham,
        staying,
        landed,
        got.reshape(2, shard_count, row_count, LANES),
    )
    return result[None]


def solution(mesh):
    chans, rows = mesh.devices.shape
    pairs = Mesh(mesh.devices.reshape(2, chans // 2, rows), ("hi", "lo", "row"))
    chan = ("hi", "lo")
    placed = (
        P(chan, "row", None),
        P(chan, "row", None),
        P(chan),
        P(chan, None),
        P(chan, None),
        P(chan, None),
        P(),
    )
    return jax.shard_map(
        on_device, mesh=pairs, in_specs=placed, out_specs=P(chan, "row", None), check_vma=False
    )
```

time: 353 us -> 300 us (0.85)
  waiting for transfers between devices: 167 us -> 103 us
  Pallas kernels: 0 us -> 38.3 us
  local copies, waits for them, and re-layouts: 43.7 us -> 21.9 us
  other arithmetic: 14.2 us -> 1.89 us
  matrix products: 36 us -> 40.3 us
    all_gather x2 -> x1, waiting for transfers between devices: 133 us -> 75.5 us  [on_device(): gathered = lax.all_gather(both, 'row', axis=0, tiled=False)]
    pallas_call x0 -> x9, Pallas kernels: none -> 38.3 us  [the longest x1 31.8 us: on_device(): pl.pallas_call(functools.partial(unpack_kernel, shard_count, sent_tiles,...]
    all_to_all x1, waiting for transfers between devices: 14.9 us -> 0.01 us  [on_device(): lax.all_to_all(blocks, ('hi', 'row'), split_axis=0, concat_axis=0, tiled=...]
    convert_element_type x5 -> x1, local copies, waits for them, and re-layouts: 12.9 us -> 1.95 us  [on_device(): lax.dynamic_slice_in_dim(running, (1 - hi) * half, half, 0).astype(BF)]
    ppermute x4, waiting for transfers between devices: 18.8 us -> 27.9 us  [swapped(): return lax.ppermute(value, 'hi', [(0, 1), (1, 0)])]
    div x2 -> x0, local copies, waits for them, and re-layouts: 6.72 us -> none  [on_device(): flipped.astype(jnp.float32) / TERMS]
    all_to_all x4 -> x0, local copies, waits for them, and re-layouts: 6.39 us -> none  [on_device(): lax.all_to_all(sent, ('row', 'hi'), split_axis=0, concat_axis=0, tiled=True)]
    reshape x2 -> x1, local copies, waits for them, and re-layouts: 4.88 us -> 0.35 us  [on_device(): blocks = columns.reshape(shard_count, row_count, 2, LANES)]
  transfers between devices with their start and end apart: 7 -> 6, of which waited for: 5 -> 3; matrix products, arithmetic and copies ran while one was open for 8% -> 5% of each run, Pallas kernels for 0% -> 0%
where the time goes in v2:
time: 300 us; the launch traced here: 299 us
  waiting for transfers between devices  103 us (34%)
  blocking collectives  54 us (18%)
  matrix products  40.3 us (13%)
  Pallas kernels  38.3 us (13%)
  between operations  25.1 us (8%)
  local copies, waits for them, and re-layouts  21.9 us (7%)
  starting transfers between devices  14.1 us (5%)
    all_gather x1, waiting for transfers between devices, on_device(): gathered = lax.all_gather(both, 'row', axis=0, tiled=False)  75.5 us
    all_to_all x2, blocking collectives, on_device(): lax.all_to_all(columns.reshape(2 * shard_count, half, 2 * LANES), ('row',...  54 us
    pallas_call x1, Pallas kernels, on_device(): pl.pallas_call(functools.partial(unpack_kernel, shard_count, sent_tiles,...  31.8 us
    ppermute x4, waiting for transfers between devices, swapped(): return lax.ppermute(value, 'hi', [(0, 1), (1, 0)])  27.9 us
    dot_general x3, matrix products, on_device(): jnp.dot(mixed_far, omegas[1], preferred_element_type=F32)  22.3 us
    dot_general x3, matrix products, on_device(): jnp.dot(mixed_own, omegas[0], preferred_element_type=F32)  18 us
    ppermute x4, starting transfers between devices, swapped(): return lax.ppermute(value, 'hi', [(0, 1), (1, 0)])  10.2 us
    scatter x1, local copies, waits for them, and re-layouts, on_device(): jnp.zeros((state_count,), jnp.int32).at[ph_order[0]].set(ph_occupation[0])  9.93 us
  transfers between devices with their start and end apart: 6, of which 3 were waited for; matrix products, arithmetic and copies ran while one was open for 5% of the time, Pallas kernels for 0%

profile of v2, /device:TPU:0, one launch (start us, length us, event | category | flops | bytes accessed | tf_op | source)
XLA Modules:
  0.0 299.0 jit_solution(17292157047832654951)
XLA Ops:
  7.3 1.1 copy-done.1
  9.2 3.2 %collective-permute-start.2 = (bf16[160,1408]{1,0:T(8,128)(2,1)S(1)}, bf16[160,1408]{1,0:T(8,128)(2,1)S(1)}, u32[]{:S(2)}, u32[]{:S(2)}) collective-permute-start(bf16[160,1408]{1,0:T(8,128)(2,1)S(1)} %pack.1), channel_id=1, source_target_pairs={{0,64},{64,0},{1,65},{65,1},{2,66},{66,2},{3,67},{67,3},{4,68},{68... | collective-permute-start | bytes 1351688 | tf_op jit(solution)/shard_map/ppermute | solution.py:157
  12.4 10.3 %collective-permute-done.2 = bf16[160,1408]{1,0:T(8,128)(2,1)S(1)} collective-permute-done((bf16[160,1408]{1,0:T(8,128)(2,1)S(1)}, bf16[160,1408]{1,0:T(8,128)(2,1)S(1)}, u32[]{:S(2)}, u32[]{:S(2)}) %collective-permute-start.2) | collective-permute-done | bytes 450592 | tf_op jit(solution)/shard_map/ppermute | solution.py:157
  23.9 9.9 %scatter_custom_fusion = s32[2560]{0:T(1024)S(1)} fusion(s32[2560]{0:T(1024)S(1)} %fusion.12, s32[2560]{0:T(1024)S(1)} %reduce.1, s32[]{:T(128)} %constant.9.clone.1), kind=kCustom, calls=%fused_computation.40 | custom fusion | bytes 10244 | tf_op jit(solution)/shard_map/scatter | solution.py:205
  34.0 3.3 %collective-permute-start.1 = (f32[2,2560]{1,0:T(2,128)S(1)}, f32[2,2560]{1,0:T(2,128)S(1)}, u32[]{:S(2)}, u32[]{:S(2)}) collective-permute-start(f32[2,2560]{1,0:T(2,128)S(1)} %add_convert_fusion), channel_id=1, source_target_pairs={{0,64},{64,0},{1,65},{65,1},{2,66},{66,2},{3,67},{67,3},{4,68},{68... | collective-permute-start | bytes 61448 | tf_op jit(solution)/shard_map/ppermute | solution.py:157
  50.3 75.5 %all-gather.3.cloned.1.call-done = bf16[32,160,1408]{2,1,0:T(8,128)(2,1)} async-done(((bf16[2,160,1408]{2,1,0:T(8,128)(2,1)}), bf16[32,160,1408]{2,1,0:T(8,128)(2,1)}) %all-gather.3.cloned.1.call-update) | async-done | bytes 14417936 | tf_op jit(solution)/shard_map/all_gather | solution.py:189
  125.9 5.1 %copy-done = bf16[32,160,1408]{2,1,0:T(8,128)(2,1)S(1)} copy-done((bf16[32,160,1408]{2,1,0:T(8,128)(2,1)S(1)}, bf16[32,160,1408]{2,1,0:T(8,128)(2,1)}, u32[]{:S(2)}) %copy-start) | copy-done | bytes 14417944
  131.0 31.8 %unpack.1 = bf16[2,2560,2560]{2,1,0:T(8,128)(2,1)} custom-call(bf16[16,2,160,1408]{3,2,1,0:T(8,128)(2,1)S(1)} %bitcast.55), custom_call_target="tpu_custom_call" | custom-call | tf_op jit(solution)/shard_map/unpack/pallas_call | solution.py:190
  162.8 6.0 %fusion.2 = f32[160,2560]{1,0:T(8,128)S(1)} fusion(bf16[160,2560]{1,0:T(8,128)(2,1)S(1)} %get-tuple-element.13, bf16[2,2560,2560]{2,1,0:T(8,128)(2,1)} %unpack.1), kind=kOutput, calls=%fused_computation.5 | convolution fusion | flops 2097152000 | bytes 15564800 | tf_op jit(solution)/shard_map/dot_general | solution.py:232
  168.8 7.0 %fusion.11.c_ref = bf16[160,2560]{1,0:T(8,128)(2,1)S(1)} fusion(f32[160,2560]{1,0:T(8,128)S(1)} %fusion.2, bf16[160,2560]{1,0:T(8,128)(2,1)S(1)} %get-tuple-element.14, bf16[2,2560,2560]{2,1,0:T(8,128)(2,1)} %unpack.1), kind=kOutput, calls=%fused_computation.14 | convolution fusion | flops 2097971200 | bytes 16384000 | tf_op jit(solution)/shard_map/dot_general | solution.py:232
  176.2 29.8 %all_to_all.15.got_ref = bf16[32,80,256]{2,1,0:T(8,128)(2,1)S(1)} all-to-all(bf16[32,80,256]{2,1,0:T(8,128)(2,1)S(1)} %bitcast.57), channel_id=1, replica_groups=mesh['hi'=2,'lo'=4,'row'=16] {'row','hi'}, dimensions={0} | all-to-all | bytes 2621440 | tf_op jit(solution)/shard_map/all_to_all | solution.py:243
  206.2 1.1 update.2
  207.3 6.0 %fusion.1 = f32[160,2560]{1,0:T(8,128)S(1)} fusion(bf16[160,2560]{1,0:T(8,128)(2,1)S(1)} %get-tuple-element.15, bf16[2,2560,2560]{2,1,0:T(8,128)(2,1)} %unpack.1), kind=kOutput, calls=%fused_computation.4 | convolution fusion | flops 2097152000 | bytes 15564800 | tf_op jit(solution)/shard_map/dot_general | solution.py:232
  213.3 7.0 %fusion.10.c_ref = bf16[160,2560]{1,0:T(8,128)(2,1)S(1)} fusion(f32[160,2560]{1,0:T(8,128)S(1)} %fusion.1, bf16[160,2560]{1,0:T(8,128)(2,1)S(1)} %get-tuple-element.16, bf16[2,2560,2560]{2,1,0:T(8,128)(2,1)} %unpack.1), kind=kOutput, calls=%fused_computation.13 | convolution fusion | flops 2097971200 | bytes 16384000 | tf_op jit(solution)/shard_map/dot_general | solution.py:232
  220.8 24.2 %all_to_all.16.got_ref = bf16[32,80,256]{2,1,0:T(8,128)(2,1)S(1)} all-to-all(bf16[32,80,256]{2,1,0:T(8,128)(2,1)S(1)} %bitcast.58), channel_id=1, replica_groups=mesh['hi'=2,'lo'=4,'row'=16] {'row','hi'}, dimensions={0} | all-to-all | bytes 2621440 | tf_op jit(solution)/shard_map/all_to_all | solution.py:243
  246.1 6.0 %fusion = f32[160,2560]{1,0:T(8,128)S(1)} fusion(bf16[160,2560]{1,0:T(8,128)(2,1)S(1)} %get-tuple-element.19, bf16[2,2560,2560]{2,1,0:T(8,128)(2,1)} %unpack.1), kind=kOutput, calls=%fused_computation.3 | convolution fusion | flops 2097152000 | bytes 15564800 | tf_op jit(solution)/shard_map/dot_general | solution.py:232
  252.1 8.2 %multiply_subtract_fusion = (f32[160,2560]{1,0:T(8,128)}, bf16[160,2560]{1,0:T(8,128)(2,1)S(1)}) fusion(f32[160,2560]{1,0:T(8,128)S(1)} %get-tuple-element.18, f32[160,2560]{1,0:T(8,128)S(1)} %fusion, bf16[160,2560]{1,0:T(8,128)(2,1)S(1)} %get-tuple-element.20, bf16[2,2560,2560]{2,1,0:T(8,128)(2,1)} %unpack.1), kind=kOutput, calls=%fused_computation.15 | convolution fusion | flops 2099200000 | bytes 19660800 | tf_op jit(solution)/shard_map/dot_general | solution.py:232
  261.1 1.3 copy.10
  262.4 3.9 %all-to-all-start.2 = ((bf16[32,160,128]{2,1,0:T(8,128)(2,1)}), bf16[32,160,128]{2,1,0:T(8,128)(2,1)S(1)}, u32[]{:S(2)}, u32[]{:S(2)}) async-start(bf16[32,160,128]{2,1,0:T(8,128)(2,1)} %bitcast.18), calls=%async_computation.2 | async-start | bytes 2621440 | tf_op jit(solution)/shard_map/all_to_all | solution.py:262
  266.4 2.0 dynamic-slice_convert_fusion
  268.3 3.3 %collective-permute-start.3 = (bf16[80,2560]{1,0:T(8,128)(2,1)}, bf16[80,2560]{1,0:T(8,128)(2,1)S(1)}, u32[]{:S(2)}, u32[]{:S(2)}) collective-permute-start(bf16[80,2560]{1,0:T(8,128)(2,1)} %dynamic-slice_convert_fusion), channel_id=1, source_target_pairs={{0,64},{64,0},{1,65},{65,1},{2,66},{66,2},{3,67},{67,3},{4,68},{68... | collective-permute-start | bytes 1228808 | tf_op jit(solution)/shard_map/ppermute | solution.py:157
  271.6 1.2 constant_dynamic-slice_fusion.stay_ref
  272.8 17.5 %collective-permute-done.3.land_ref = bf16[80,2560]{1,0:T(8,128)(2,1)S(1)} collective-permute-done((bf16[80,2560]{1,0:T(8,128)(2,1)}, bf16[80,2560]{1,0:T(8,128)(2,1)S(1)}, u32[]{:S(2)}, u32[]{:S(2)}) %collective-permute-start.3) | collective-permute-done | bytes 409632 | tf_op jit(solution)/shard_map/ppermute | solution.py:157
  290.4 1.8 finish.1
  (45 shorter events, 7.1 us)
Async XLA Ops:
  6.5 119.3 %all-gather.3.cloned.1.call-start = ((), (), s32[]{:S(2)}) async-start(), calls=%async_computation.3 | async-start | bytes 15319040 | tf_op jit(solution)/shard_map/all_gather | solution.py:189
  7.3 1.1 copy-start.1
  9.2 14.6 %copy-start.3 = (s32[1,2560]{1,0:T(1,128)S(1)}, s32[1,2560]{1,0:T(1,128)}, u32[]{:S(2)}) copy-start(s32[1,2560]{1,0:T(1,128)} %param.11) | copy-start | bytes 30724
  9.2 14.7 %copy-start.4 = (s32[1,2560]{1,0:T(1,128)S(1)}, s32[1,2560]{1,0:T(1,128)}, u32[]{:S(2)}) copy-start(s32[1,2560]{1,0:T(1,128)} %param.12) | copy-start | bytes 30724
  9.2 24.7 %copy-start.5 = (s32[1,2560]{1,0:T(1,128)S(1)}, s32[1,2560]{1,0:T(1,128)}, u32[]{:S(2)}) copy-start(s32[1,2560]{1,0:T(1,128)} %param.10) | copy-start | bytes 30724
  9.2 28.1 %copy-start.2 = (bf16[1,160,2560]{2,1,0:T(8,128)(2,1)S(1)}, bf16[1,160,2560]{2,1,0:T(8,128)(2,1)}, u32[]{:S(2)}) copy-start(bf16[1,160,2560]{2,1,0:T(8,128)(2,1)} %param.8) | copy-start | bytes 2457604
  9.2 13.6 %collective-permute-start.2 = (bf16[160,1408]{1,0:T(8,128)(2,1)S(1)}, bf16[160,1408]{1,0:T(8,128)(2,1)S(1)}, u32[]{:S(2)}, u32[]{:S(2)}) collective-permute-start(bf16[160,1408]{1,0:T(8,128)(2,1)S(1)} %pack.1), channel_id=1, source_target_pairs={{0,64},{64,0},{1,65},{65,1},{2,66},{66,2},{3,67},{67,3},{4,68},{68... | collective-permute-start | bytes 1351688 | tf_op jit(solution)/shard_map/ppermute | solution.py:157
  23.8 14.2 %copy-start.6 = (f32[8,2]{0,1:T(2,128)S(1)}, f32[8,2]{0,1:T(2,128)}, u32[]{:S(2)}) copy-start(f32[8,2]{0,1:T(2,128)} %param.13) | copy-start | bytes 196
  34.0 15.5 %collective-permute-start.1 = (f32[2,2560]{1,0:T(2,128)S(1)}, f32[2,2560]{1,0:T(2,128)S(1)}, u32[]{:S(2)}, u32[]{:S(2)}) collective-permute-start(f32[2,2560]{1,0:T(2,128)S(1)} %add_convert_fusion), channel_id=1, source_target_pairs={{0,64},{64,0},{1,65},{65,1},{2,66},{66,2},{3,67},{67,3},{4,68},{68... | collective-permute-start | bytes 61448 | tf_op jit(solution)/shard_map/ppermute | solution.py:157
  37.7 11.9 %collective-permute-start = (bf16[80,2560]{1,0:T(8,128)(2,1)S(1)}, bf16[80,2560]{1,0:T(8,128)(2,1)S(1)}, u32[]{:S(2)}, u32[]{:S(2)}) collective-permute-start(bf16[80,2560]{1,0:T(8,128)(2,1)S(1)} %constant_dynamic-slice_fusion.3), channel_id=1, source_target_pairs={{0,64},{64,0},{1,65},{65,1},{2,66},{66,2},{3,67},{67,3},{4,68},{68... | collective-permute-start | bytes 1228808 | tf_op jit(solution)/shard_map/ppermute | solution.py:157
  125.9 5.1 %copy-start = (bf16[32,160,1408]{2,1,0:T(8,128)(2,1)S(1)}, bf16[32,160,1408]{2,1,0:T(8,128)(2,1)}, u32[]{:S(2)}) copy-start(bf16[32,160,1408]{2,1,0:T(8,128)(2,1)} %all-gather.3.cloned.1.call-done) | copy-start | bytes 43253764
  262.4 28.0 %all-to-all-start.2 = ((bf16[32,160,128]{2,1,0:T(8,128)(2,1)}), bf16[32,160,128]{2,1,0:T(8,128)(2,1)S(1)}, u32[]{:S(2)}, u32[]{:S(2)}) async-start(bf16[32,160,128]{2,1,0:T(8,128)(2,1)} %bitcast.18), calls=%async_computation.2 | async-start | bytes 2621440 | tf_op jit(solution)/shard_map/all_to_all | solution.py:262
  268.3 22.0 %collective-permute-start.3 = (bf16[80,2560]{1,0:T(8,128)(2,1)}, bf16[80,2560]{1,0:T(8,128)(2,1)S(1)}, u32[]{:S(2)}, u32[]{:S(2)}) collective-permute-start(bf16[80,2560]{1,0:T(8,128)(2,1)} %dynamic-slice_convert_fusion), channel_id=1, source_target_pairs={{0,64},{64,0},{1,65},{65,1},{2,66},{66,2},{3,67},{67,3},{4,68},{68... | collective-permute-start | bytes 1228808 | tf_op jit(solution)/shard_map/ppermute | solution.py:157
Sparse Core Ops, SparseCore 0:
  24.0 101.8 all-gather.2

commit v3 on v1

v3 whole, which is shorter than its diff:
```python
import functools

import jax
import jax.numpy as jnp
from jax import lax
from jax.experimental import pallas as pl
from jax.experimental.pallas import tpu as pltpu
from jax.sharding import Mesh, PartitionSpec as P

TERMS = 3
LANES = 128
STEP = 32
BF = jnp.bfloat16
F32 = jnp.float32
VMEM = pl.BlockSpec(memory_space=pltpu.VMEM)
SMEM = pl.BlockSpec(memory_space=pltpu.SMEM)
HBM = pl.BlockSpec(memory_space=pltpu.HBM)


def tile_at(index):
    return pl.ds(pl.multiple_of(index * LANES, LANES), LANES)


def pack_kernel(sent_tiles, tiles, scalars, gen_ref, out_ref):
    start, live = scalars[0], scalars[1]
    for group in range(gen_ref.shape[0] // STEP):
        rows = pl.ds(group * STEP, STEP)
        first_row = start + group * STEP
        diagonal = first_row // LANES
        row_at = first_row + lax.broadcasted_iota(jnp.int32, (STEP, LANES), 0)
        for apart in range(sent_tiles):
            tile = lax.rem(diagonal + apart, tiles)
            column_at = tile * LANES + lax.broadcasted_iota(jnp.int32, (STEP, LANES), 1)
            alive = (row_at < live) & (column_at < live)
            value = gen_ref[rows, tile_at(tile)].astype(F32)
            out_ref[rows, apart * LANES : (apart + 1) * LANES] = jnp.where(
                alive, value, 0.0
            ).astype(BF)


def shifted(value, shift):
    shift = shift % LANES
    return pltpu.roll(value, shift, 1) if shift else value


def lane_index():
    return lax.broadcasted_iota(jnp.int32, (1, LANES), 1)


def laid_out(pieces, half, tile):
    low = tile * LANES
    result = None
    for piece in range(low // half, (low + LANES - 1) // half + 1):
        begin = piece * half - low
        value = pieces(piece, begin)
        result = value if result is None else jnp.where(lane_index() >= begin, value, result)
    return result


def mix(x0, x1, own_ref, far_ref, mixed, half, tile, tiles):
    at = slice(tile * LANES, (tile + 1) * LANES)
    places = [at]
    if (tile + tiles + 1) * LANES <= mixed.shape[2]:
        places.append(slice((tile + tiles) * LANES, (tile + tiles + 1) * LANES))
    for which, weights in enumerate((own_ref, far_ref)):
        top = (x0 * weights[0:1, at] + x1 * weights[1:2, at]).astype(BF)
        low = (x0 * weights[2:3, at] + x1 * weights[3:4, at]).astype(BF)
        for place in places:
            mixed[which, :half, place] = top
            mixed[which, half:, place] = low


def product(got_ref, mixed, total, held, sems, tiles):
    pairs = tiles // 2
    blocks = got_ref.shape[0]
    per_chunk = blocks // 2

    def step(index, carry):
        which = index // pairs
        pair = lax.rem(index, pairs)

        @pl.when(lax.rem(index, pairs // 2) == 0)
        def _():
            chunk = lax.rem(index // (pairs // 2), 2)

            @pl.loop(0, per_chunk)
            def _(k):
                block_copy(got_ref, held, sems, which, chunk * per_chunk + k).wait()

        even = pl.multiple_of(pair * 2 * LANES, 2 * LANES)
        odd = pl.multiple_of(even + LANES, LANES)

        def rows(start, low, high):
            return held[which, pl.ds(start, LANES), low * LANES : high * LANES]

        def left(apart, count):
            at = pl.multiple_of(even + apart * LANES, LANES)
            return mixed[which, :, pl.ds(at, count * LANES)]

        def add(apart, count, value):
            at = pl.multiple_of(even + apart * LANES, LANES)
            total[:, pl.ds(at, count * LANES)] += value

        def straight(a, w):
            return jnp.dot(a, w, preferred_element_type=F32)

        def turned(a, w):
            return lax.dot_general(a, w, (((1,), (1,)), ((), ())), preferred_element_type=F32)

        span = pairs
        both = jnp.concatenate([rows(even, 1, span + 1), rows(odd, 0, span)], 0)
        add(1, span, straight(left(0, 2), both))
        both = jnp.concatenate([rows(even, 2, span), rows(odd, 1, span - 1)], 0)
        add(0, 2, -turned(left(2, span - 2), both))
        add(0, 1, straight(left(0, 1), rows(even, 0, 1)) - turned(left(1, 1), rows(even, 1, 2)))
        add(1, 1, -turned(left(span, 1), rows(odd, span - 1, span)))
        add(span + 1, 1, straight(left(1, 1), rows(odd, span, span + 1)))
        return carry

    lax.fori_loop(0, 2 * pairs, step, 0)


def block_copy(got_ref, held, sems, which, block):
    rows = got_ref.shape[2]
    at = pl.multiple_of(block * rows, rows)
    return pltpu.make_async_copy(
        got_ref.at[block, which], held.at[which, pl.ds(at, rows)], sems.at[which, block]
    )


def begin(got_ref, held, sems):
    for which in range(2):

        @pl.loop(0, got_ref.shape[0])
        def _(block):
            block_copy(got_ref, held, sems, which, block).start()


def folded(total, tile, tiles):
    at = slice(tile * LANES, (tile + 1) * LANES)
    value = total[:, at]
    if (tile + tiles + 1) * LANES <= total.shape[1]:
        value = value + total[:, (tile + tiles) * LANES : (tile + tiles + 1) * LANES]
    return value.astype(BF)


def pack_columns(c_ref, columns, half):
    count = c_ref.shape[1] // half
    rest = c_ref.shape[0] - LANES
    for tile in range(c_ref.shape[1] // LANES):
        block = c_ref[:LANES, tile * LANES : (tile + 1) * LANES].astype(F32).T.astype(BF)
        step = 16
        for k in range(LANES // step):
            row = tile * LANES + k * step
            columns[row // half, row % half : row % half + step, :] = block[k * step : (k + 1) * step]
    for piece in range(count):
        tile, off = divmod(piece * half, LANES)
        tail = slice(LANES, LANES + rest)
        value = shifted(c_ref[tail, tile * LANES : (tile + 1) * LANES].astype(F32), -off)
        if off + half > LANES:
            more = c_ref[tail, (tile + 1) * LANES : (tile + 2) * LANES].astype(F32)
            value = jnp.where(lane_index() < LANES - off, value, shifted(more, -off))
        columns[piece, half : half + rest, :] = value.astype(BF)


def flipped_tiles(got_ref, turned, half, tile):
    rest = 2 * half - LANES
    group = LANES // rest
    kept = half - rest

    def near(s, begin):
        return shifted(got_ref[s, :half, :].astype(F32), begin)

    def far(s, begin):
        front = shifted(got_ref[s, :half, :].astype(F32), begin - half)
        back = turned[s // group, :half, :]
        back = shifted(back, begin + kept - rest * (s % group))
        return jnp.where(lane_index() >= begin + kept, back, front)

    def far_safe(s, begin):
        return far(s, begin)

    return laid_out(near, half, tile), laid_out(far_safe, half, tile)


def turn_rest(got_ref, turned, half):
    rest = 2 * half - LANES
    group = LANES // rest
    for k in range(got_ref.shape[0] // group):
        block = jnp.concatenate(
            [got_ref[k * group + m, half : half + rest, :].astype(F32) for m in range(group)], 0
        )
        turned[k] = block.T


def finish_products(c_out, total, tiles):
    for tile in range(tiles):
        c_out[:, tile * LANES : (tile + 1) * LANES] = folded(total, tile, tiles)


def first_kernel(
    half, tiles, x_ref, own_ref, far_ref, got_ref, c_out, columns, mixed, total, held, sems
):
    begin(got_ref, held, sems)
    for tile in range(tiles):
        at = slice(tile * LANES, (tile + 1) * LANES)
        x0, x1 = x_ref[:half, at].astype(F32), x_ref[half:, at].astype(F32)
        mix(x0, x1, own_ref, far_ref, mixed, half, tile, tiles)
    total[...] = jnp.zeros_like(total)
    product(got_ref, mixed, total, held, sems, tiles)
    finish_products(c_out, total, tiles)
    pack_columns(c_out, columns, half)


def update(half, tiles, scale, c_ref, back_ref, own_ref, far_ref, mixed, turned, keep):
    turn_rest(back_ref, turned, half)
    for tile in range(tiles):
        at = slice(tile * LANES, (tile + 1) * LANES)
        xs = []
        for channel, flipped in enumerate(flipped_tiles(back_ref, turned, half, tile)):
            rows = slice(channel * half, (channel + 1) * half)
            increment = (c_ref[rows, at].astype(F32) + flipped) * scale
            keep(rows, at, increment)
            xs.append(increment.astype(BF).astype(F32))
        mix(xs[0], xs[1], own_ref, far_ref, mixed, half, tile, tiles)


def middle_kernel(
    half, tiles, scale, c_ref, back_ref, own_ref, far_ref, got_ref, c_out, run_out, columns,
    mixed, total, held, sems, turned,
):
    begin(got_ref, held, sems)

    def keep(rows, at, increment):
        run_out[rows, at] = increment

    update(half, tiles, scale, c_ref, back_ref, own_ref, far_ref, mixed, turned, keep)
    total[...] = jnp.zeros_like(total)
    product(got_ref, mixed, total, held, sems, tiles)
    finish_products(c_out, total, tiles)
    pack_columns(c_out, columns, half)


def last_kernel(
    half, tiles, scale, last_scale, first_ref, c_ref, back_ref, run_ref, own_ref, far_ref, got_ref,
    leave, stay, columns, mixed, total, held, sems, turned, run,
):
    begin(got_ref, held, sems)

    def keep(rows, at, increment):
        run[rows, at] = run_ref[rows, at] + increment

    update(half, tiles, scale, c_ref, back_ref, own_ref, far_ref, mixed, turned, keep)
    total[...] = jnp.zeros_like(total)
    product(got_ref, mixed, total, held, sems, tiles)
    first = first_ref[0] != 0
    filler = jnp.zeros((LANES - half, LANES), F32)
    for tile in range(tiles):
        at = slice(tile * LANES, (tile + 1) * LANES)
        value = folded(total, tile, tiles).astype(F32)
        for channel in range(2):
            block = jnp.concatenate([value[channel * half : (channel + 1) * half], filler])
            columns[channel, at, :] = block.T.astype(BF)
        both = run[:, at] + value * last_scale
        leave[:, at] = jnp.where(first, both[half:], both[:half]).astype(BF)
        stay[:, at] = jnp.where(first, both[:half], both[half:])


def end_kernel(half, scale, first_ref, ham_ref, stay_ref, land_ref, got_ref, out_ref):
    first = first_ref[0] != 0

    def piece(s, begin):
        return shifted(got_ref[s % 2, s // 2].astype(F32), begin)

    for tile in range(ham_ref.shape[1] // LANES):
        at = slice(tile * LANES, (tile + 1) * LANES)
        total = ham_ref[:, at].astype(F32) + laid_out(piece, half, tile) * scale
        stay, land = stay_ref[:, at], land_ref[:, at].astype(F32)
        out_ref[:half, at] = total[:half] + jnp.where(first, stay, land)
        out_ref[half:, at] = total[half:] + jnp.where(first, land, stay)


def call(kernel, out_shape, specs, name, scratch=(), cost=None):
    single = not isinstance(out_shape, (list, tuple))
    return pl.pallas_call(
        kernel,
        out_shape=out_shape,
        in_specs=specs,
        out_specs=VMEM if single else [VMEM] * len(out_shape),
        scratch_shapes=scratch,
        compiler_params=pltpu.CompilerParams(vmem_limit_bytes=(40 if scratch else 16) << 20),
        cost_estimate=cost,
        name=name,
    )


def swapped(value):
    return lax.ppermute(value, "hi", [(0, 1), (1, 0)])


def on_device(
    generator, hamiltonian, live_states, pp_occupation, ph_occupation, ph_order, recoupling
):
    row_count = generator.shape[1]
    state_count = generator.shape[2]
    half = row_count // 2
    shard_count = lax.axis_size("row")
    tiles = state_count // LANES
    sent_tiles = tiles // 2 + 1
    hi = lax.axis_index("hi")
    lo = lax.axis_index("lo")
    my_shard = lax.axis_index("row")
    first = hi == 0
    shape = jax.ShapeDtypeStruct
    r0 = recoupling[lo]
    r1 = recoupling[lo + lax.axis_size("lo")]
    positions = jnp.arange(state_count, dtype=jnp.int32)
    live_count = live_states[0]
    column_alive = positions < live_count
    row_alive = my_shard * row_count + jnp.arange(row_count, dtype=jnp.int32) < live_count
    block_alive = row_alive[:, None] & column_alive[None, :]

    share = call(
        functools.partial(pack_kernel, sent_tiles, tiles),
        shape((row_count, sent_tiles * LANES), BF),
        [SMEM, VMEM],
        "pack",
    )(jnp.stack([my_shard * row_count, live_count]), generator[0])
    both = jnp.stack([share, swapped(share)])
    gathered = lax.all_gather(both, "row", axis=0, tiled=False)
    pp = jnp.where(column_alive, pp_occupation[0], 0)
    ph = jnp.zeros((state_count,), jnp.int32).at[ph_order[0]].set(ph_occupation[0])
    ph = jnp.where(column_alive, ph, 0)
    mine = jnp.stack([pp, ph]).astype(F32)
    other = swapped(mine)
    d0, n0 = jnp.where(first, mine, other)
    d1, n1 = jnp.where(first, other, mine)
    a0 = d0 + r0[0] ** 3 * n0 + r1[1] ** 3 * n1
    a1 = d1 + r1[0] ** 3 * n1 + r0[1] ** 3 * n0
    p = r0[0] ** 2 * r0[1] * n0 + r1[1] ** 2 * r1[0] * n1
    q = r1[0] ** 2 * r1[1] * n1 + r0[1] ** 2 * r0[0] * n0
    zero_set = jnp.stack([a0, p, p, q])
    one_set = jnp.stack([p, q, q, a1])
    own_set = jnp.where(first, zero_set, one_set)
    far_set = jnp.where(first, one_set, zero_set)

    own_ham = jnp.where(block_alive, hamiltonian[0], jnp.zeros_like(hamiltonian[0]))
    keep = lax.dynamic_slice_in_dim(own_ham, hi * half, half, 0)
    gone = lax.dynamic_slice_in_dim(own_ham, (1 - hi) * half, half, 0)
    came = swapped(gone)
    current = jnp.concatenate([jnp.where(first, keep, came), jnp.where(first, came, keep)])

    wide = (tiles + sent_tiles - 1) * LANES
    rest = row_count - LANES
    destinations = 2 * shard_count
    scratch = [
        pltpu.VMEM((2, row_count, wide), BF),
        pltpu.VMEM((row_count, wide), F32),
        pltpu.VMEM((2, state_count, sent_tiles * LANES), BF),
        pltpu.SemaphoreType.DMA((2, shard_count)),
    ]
    more = [pltpu.VMEM((destinations * rest // LANES, LANES, LANES), F32)]
    c_shape = shape((row_count, state_count), BF)
    run_shape = shape((row_count, state_count), F32)
    sent_shape = shape((destinations, half + rest, LANES), BF)
    cost = pl.CostEstimate(
        flops=4 * row_count * state_count * state_count,
        bytes_accessed=gathered.size * 2,
        transcendentals=0,
    )

    def exchanged(columns):
        return lax.all_to_all(columns, ("row", "hi"), split_axis=0, concat_axis=0, tiled=True)

    combined, columns = call(
        functools.partial(first_kernel, half, tiles),
        [c_shape, sent_shape],
        [VMEM] * 3 + [HBM],
        "first",
        scratch,
        cost,
    )(current, own_set, far_set, gathered)
    back = exchanged(columns)
    combined, running, columns = call(
        functools.partial(middle_kernel, half, tiles, -1.0),
        [c_shape, run_shape, sent_shape],
        [VMEM] * 4 + [HBM],
        "middle",
        scratch + more,
        cost,
    )(combined, back, own_set, far_set, gathered)
    back = exchanged(columns)
    which = first.astype(jnp.int32)[None]
    leaving, staying, blocks = call(
        functools.partial(last_kernel, half, tiles, -0.5, -1.0 / TERMS),
        [
            shape((half, state_count), BF),
            shape((half, state_count), F32),
            shape((2, state_count, LANES), BF),
        ],
        [SMEM] + [VMEM] * 5 + [HBM],
        "last",
        scratch + more + [pltpu.VMEM((row_count, state_count), F32)],
        cost,
    )(which, combined, back, running, own_set, far_set, gathered)
    landed = swapped(leaving)
    got = lax.all_to_all(
        blocks.reshape(destinations, row_count, LANES),
        ("hi", "row"),
        split_axis=0,
        concat_axis=0,
        tiled=True,
    )
    result = call(
        functools.partial(end_kernel, half, -1.0 / TERMS),
        shape((row_count, state_count), F32),
        [SMEM] + [VMEM] * 4,
        "finish",
    )(which, own_ham, staying, landed, got.reshape(2, shard_count, row_count, LANES))
    return result[None]


def solution(mesh):
    chans, rows = mesh.devices.shape
    pairs = Mesh(mesh.devices.reshape(2, chans // 2, rows), ("hi", "lo", "row"))
    chan = ("hi", "lo")
    placed = (
        P(chan, "row", None),
        P(chan, "row", None),
        P(chan),
        P(chan, None),
        P(chan, None),
        P(chan, None),
        P(),
    )
    return jax.shard_map(
        on_device, mesh=pairs, in_specs=placed, out_specs=P(chan, "row", None), check_vma=False
    )
```

time: 353 us -> 256 us (0.73)
  Pallas kernels: 0 us -> 43.2 us
  waiting for transfers between devices: 167 us -> 124 us
  matrix products: 36 us -> 0 us
  blocking collectives: 54 us -> 25.6 us
  local copies, waits for them, and re-layouts: 43.7 us -> 17.5 us
  other arithmetic: 14.2 us -> 1.88 us
  starting transfers between devices: 13.6 us -> 18.3 us
    all_gather x2 -> x1, waiting for transfers between devices: 133 us -> 76.3 us  [on_device(): gathered = lax.all_gather(both, 'row', axis=0, tiled=False)]
    pallas_call x0 -> x5, Pallas kernels: none -> 43.2 us  [the longest x1 13.6 us: on_device(): call(functools.partial(middle_kernel, half, tiles, -1.0), [c_shape, run_s...]
    dot_general x6 -> x0, matrix products: 36 us -> none  [the longest x3 22.7 us: on_device(): jnp.dot(mix(wide, own_set), full_own, preferred_element_type=jnp.float32)]
    all_to_all x2 -> x1, blocking collectives: 54 us -> 25.6 us  [exchanged(): lax.all_to_all(columns, ('row', 'hi'), split_axis=0, concat_axis=0, tiled...]
    convert_element_type x5 -> x0, local copies, waits for them, and re-layouts: 12.9 us -> none  [the longest x4 12.8 us: on_device(): flipped.astype(jnp.float32)]
    ppermute x4, waiting for transfers between devices: 18.8 us -> 30.9 us  [swapped(): return lax.ppermute(value, 'hi', [(0, 1), (1, 0)])]
    div x2 -> x0, local copies, waits for them, and re-layouts: 6.72 us -> none  [on_device(): flipped.astype(jnp.float32) / TERMS]
    all_to_all x4 -> x0, local copies, waits for them, and re-layouts: 6.39 us -> none  [on_device(): lax.all_to_all(sent, ('row', 'hi'), split_axis=0, concat_axis=0, tiled=True)]
  transfers between devices with their start and end apart: 7 -> 7, of which waited for: 5 -> 5; matrix products, arithmetic and copies ran while one was open for 8% -> 4% of each run, Pallas kernels for 0% -> 0%
where the time goes in v3:
time: 256 us; the launch traced here: 255 us
  waiting for transfers between devices  124 us (48%)
  Pallas kernels  43.2 us (17%)
  blocking collectives  25.6 us (10%)
  between operations  24.6 us (10%)
  starting transfers between devices  18.3 us (7%)
  local copies, waits for them, and re-layouts  17.5 us (7%)
    all_gather x1, waiting for transfers between devices, on_device(): gathered = lax.all_gather(both, 'row', axis=0, tiled=False)  76.3 us
    ppermute x4, waiting for transfers between devices, swapped(): return lax.ppermute(value, 'hi', [(0, 1), (1, 0)])  30.9 us
    all_to_all x1, blocking collectives, exchanged(): lax.all_to_all(columns, ('row', 'hi'), split_axis=0, concat_axis=0, tiled...  25.6 us
    all_to_all x1, waiting for transfers between devices, exchanged(): lax.all_to_all(columns, ('row', 'hi'), split_axis=0, concat_axis=0, tiled...  16.6 us
    pallas_call x1, Pallas kernels, on_device(): call(functools.partial(middle_kernel, half, tiles, -1.0), [c_shape, run_s...  13.6 us
    pallas_call x1, Pallas kernels, on_device(): call(functools.partial(last_kernel, half, tiles, -0.5, -1.0 / TERMS), [sh...  13.6 us
    pallas_call x1, Pallas kernels, on_device(): call(functools.partial(first_kernel, half, tiles), [c_shape, sent_shape],...  13.5 us
    ppermute x4, starting transfers between devices, swapped(): return lax.ppermute(value, 'hi', [(0, 1), (1, 0)])  10.3 us
  transfers between devices with their start and end apart: 7, of which 5 were waited for; matrix products, arithmetic and copies ran while one was open for 4% of the time, Pallas kernels for 0%

profile of v3, /device:TPU:0, one launch (start us, length us, event | category | flops | bytes accessed | tf_op | source)
XLA Modules:
  0.0 255.0 jit_solution(3354849017754476544)
XLA Ops:
  7.3 1.1 copy-done.4
  8.4 0.8 pack.1
  9.2 3.2 %collective-permute-start.2 = (bf16[160,1408]{1,0:T(8,128)(2,1)S(1)}, bf16[160,1408]{1,0:T(8,128)(2,1)S(1)}, u32[]{:S(2)}, u32[]{:S(2)}) collective-permute-start(bf16[160,1408]{1,0:T(8,128)(2,1)S(1)} %pack.1), channel_id=1, source_target_pairs={{0,64},{64,0},{1,65},{65,1},{2,66},{66,2},{3,67},{67,3},{4,68},{68... | collective-permute-start | bytes 1351688 | tf_op jit(solution)/shard_map/ppermute | solution.py:298
  12.4 10.3 %collective-permute-done.2 = bf16[160,1408]{1,0:T(8,128)(2,1)S(1)} collective-permute-done((bf16[160,1408]{1,0:T(8,128)(2,1)S(1)}, bf16[160,1408]{1,0:T(8,128)(2,1)S(1)}, u32[]{:S(2)}, u32[]{:S(2)}) %collective-permute-start.2) | collective-permute-done | bytes 450592 | tf_op jit(solution)/shard_map/ppermute | solution.py:298
  22.8 1.0 pad_maximum_fusion
  23.9 9.9 %scatter_custom_fusion = s32[2560]{0:T(1024)S(1)} fusion(s32[2560]{0:T(1024)S(1)} %fusion, s32[2560]{0:T(1024)S(1)} %reduce.1, s32[]{:T(128)} %constant.8.clone.1), kind=kCustom, calls=%fused_computation.24 | custom fusion | bytes 10244 | tf_op jit(solution)/shard_map/scatter | solution.py:332
  34.0 3.3 %collective-permute-start.1 = (f32[2,2560]{1,0:T(2,128)S(1)}, f32[2,2560]{1,0:T(2,128)S(1)}, u32[]{:S(2)}, u32[]{:S(2)}) collective-permute-start(f32[2,2560]{1,0:T(2,128)S(1)} %add_convert_fusion), channel_id=1, source_target_pairs={{0,64},{64,0},{1,65},{65,1},{2,66},{66,2},{3,67},{67,3},{4,68},{68... | collective-permute-start | bytes 61448 | tf_op jit(solution)/shard_map/ppermute | solution.py:298
  49.5 76.3 %all-gather.3.cloned.1.call-done = bf16[32,160,1408]{2,1,0:T(8,128)(2,1)} async-done(((bf16[2,160,1408]{2,1,0:T(8,128)(2,1)}), bf16[32,160,1408]{2,1,0:T(8,128)(2,1)}) %all-gather.3.cloned.1.call-update) | async-done | bytes 14417936 | tf_op jit(solution)/shard_map/all_gather | solution.py:330
  125.9 13.5 %first.1 = (bf16[160,2560]{1,0:T(8,128)(2,1)S(1)}, bf16[32,112,128]{2,1,0:T(8,128)(2,1)S(1)}) custom-call(bf16[160,2560]{1,0:T(8,128)(2,1)S(1)} %pad_maximum_fusion.1.x_ref, f32[4,2560]{1,0:T(4,128)S(1)} %get-tuple-element.24.own_ref, f32[4,2560]{1,0:T(4,128)S(1)} %get-tuple-element.23.far_ref, bf16[16,2,160,1408]{3,2,1,0:T(8,128)(2,1)} %bitcast.27), custom_call_target="tpu_custom_call" | custom-call | flops 4194304000 | bytes 14417920 | tf_op jit(solution)/shard_map/first/pallas_call | solution.py:375
  139.4 25.6 %all_to_all.15.back_ref = bf16[32,112,128]{2,1,0:T(8,128)(2,1)S(1)} all-to-all(bf16[32,112,128]{2,1,0:T(8,128)(2,1)S(1)} %get-tuple-element.14), channel_id=1, replica_groups=mesh['hi'=2,'lo'=4,'row'=16] {'row','hi'}, dimensions={0} | all-to-all | bytes 1835008 | tf_op jit(solution)/shard_map/all_to_all | solution.py:373
  164.9 13.6 %middle.1 = (bf16[160,2560]{1,0:T(8,128)(2,1)S(1)}, f32[160,2560]{1,0:T(8,128)S(1)}, bf16[32,112,128]{2,1,0:T(8,128)(2,1)S(1)}) custom-call(bf16[160,2560]{1,0:T(8,128)(2,1)S(1)} %get-tuple-element.13.c_ref, bf16[32,112,128]{2,1,0:T(8,128)(2,1)S(1)} %all_to_all.15.back_ref, f32[4,2560]{1,0:T(4,128)S(1)} %get-tuple-element.24.own_ref, ...), custom_call_target="tpu_custom_call" | custom-call | flops 4194304000 | bytes 14417920 | tf_op jit(solution)/shard_map/middle/pallas_call | solution.py:384
  178.5 0.9 copy-done.1
  179.4 0.9 copy-done.5
  180.3 3.9 %all-to-all-start.1 = ((bf16[32,112,128]{2,1,0:T(8,128)(2,1)}), bf16[32,112,128]{2,1,0:T(8,128)(2,1)S(1)}, u32[]{:S(2)}, u32[]{:S(2)}) async-start(bf16[32,112,128]{2,1,0:T(8,128)(2,1)} %copy-done.1), calls=%async_computation.1 | async-start | bytes 1835008 | tf_op jit(solution)/shard_map/all_to_all | solution.py:373
  184.3 16.6 %all-to-all-done.1.back_ref = bf16[32,112,128]{2,1,0:T(8,128)(2,1)S(1)} async-done(((bf16[32,112,128]{2,1,0:T(8,128)(2,1)}), bf16[32,112,128]{2,1,0:T(8,128)(2,1)S(1)}, u32[]{:S(2)}, u32[]{:S(2)}) %all-to-all-start.1) | async-done | bytes 917536 | tf_op jit(solution)/shard_map/all_to_all | solution.py:373
  200.9 1.1 copy-done.6
  202.0 13.6 %last.1 = (bf16[80,2560]{1,0:T(8,128)(2,1)S(1)}, f32[80,2560]{1,0:T(8,128)S(1)}, bf16[2,2560,128]{2,1,0:T(8,128)(2,1)S(1)}) custom-call(s32[1]{0:T(128)} %bitcast.first_ref, bf16[160,2560]{1,0:T(8,128)(2,1)S(1)} %copy-done.6, bf16[32,112,128]{2,1,0:T(8,128)(2,1)S(1)} %all-to-all-done.1.back_ref, f32[160,2560]{1,0:T(8,128)S(1)} %get-tuple-element.17.run_ref, ...), custom_call_target="tpu_custom_call" | custom-call | flops 4194304000 | bytes 14417920 | tf_op jit(solution)/shard_map/last/pallas_call | solution.py:394
  215.6 1.0 copy-done
  216.7 0.9 copy-done.2
  217.6 0.8 copy-done.7
  218.3 4.1 %all-to-all-start.2 = ((bf16[32,160,128]{2,1,0:T(8,128)(2,1)}), bf16[32,160,128]{2,1,0:T(8,128)(2,1)S(1)}, u32[]{:S(2)}, u32[]{:S(2)}) async-start(bf16[32,160,128]{2,1,0:T(8,128)(2,1)} %bitcast.25), calls=%async_computation.2 | async-start | bytes 2621440 | tf_op jit(solution)/shard_map/all_to_all | solution.py:407
  222.4 3.4 %collective-permute-start.3 = (bf16[80,2560]{1,0:T(8,128)(2,1)}, bf16[80,2560]{1,0:T(8,128)(2,1)S(1)}, u32[]{:S(2)}, u32[]{:S(2)}) collective-permute-start(bf16[80,2560]{1,0:T(8,128)(2,1)} %copy-done.7), channel_id=1, source_target_pairs={{0,64},{64,0},{1,65},{65,1},{2,66},{66,2},{3,67},{67,3},{4,68},{68... | collective-permute-start | bytes 1228808 | tf_op jit(solution)/shard_map/ppermute | solution.py:298
  225.8 20.5 %collective-permute-done.3.land_ref = bf16[80,2560]{1,0:T(8,128)(2,1)S(1)} collective-permute-done((bf16[80,2560]{1,0:T(8,128)(2,1)}, bf16[80,2560]{1,0:T(8,128)(2,1)S(1)}, u32[]{:S(2)}, u32[]{:S(2)}) %collective-permute-start.3) | collective-permute-done | bytes 409632 | tf_op jit(solution)/shard_map/ppermute | solution.py:298
  246.3 1.8 finish.1
  (43 shorter events, 2.1 us)
Async XLA Ops:
  6.5 119.3 %all-gather.3.cloned.1.call-start = ((), (), s32[]{:S(2)}) async-start(), calls=%async_computation.3 | async-start | bytes 15319040 | tf_op jit(solution)/shard_map/all_gather | solution.py:330
  7.3 1.1 copy-start.4
  9.2 14.6 %copy-start.9 = (s32[1,2560]{1,0:T(1,128)S(1)}, s32[1,2560]{1,0:T(1,128)}, u32[]{:S(2)}) copy-start(s32[1,2560]{1,0:T(1,128)} %param.11) | copy-start | bytes 30724
  9.2 14.7 %copy-start.10 = (s32[1,2560]{1,0:T(1,128)S(1)}, s32[1,2560]{1,0:T(1,128)}, u32[]{:S(2)}) copy-start(s32[1,2560]{1,0:T(1,128)} %param.12) | copy-start | bytes 30724
  9.2 24.7 %copy-start.11 = (s32[1,2560]{1,0:T(1,128)S(1)}, s32[1,2560]{1,0:T(1,128)}, u32[]{:S(2)}) copy-start(s32[1,2560]{1,0:T(1,128)} %param.10) | copy-start | bytes 30724
  9.2 28.1 %copy-start.8 = (bf16[1,160,2560]{2,1,0:T(8,128)(2,1)S(1)}, bf16[1,160,2560]{2,1,0:T(8,128)(2,1)}, u32[]{:S(2)}) copy-start(bf16[1,160,2560]{2,1,0:T(8,128)(2,1)} %param.8) | copy-start | bytes 2457604
  9.2 13.6 %collective-permute-start.2 = (bf16[160,1408]{1,0:T(8,128)(2,1)S(1)}, bf16[160,1408]{1,0:T(8,128)(2,1)S(1)}, u32[]{:S(2)}, u32[]{:S(2)}) collective-permute-start(bf16[160,1408]{1,0:T(8,128)(2,1)S(1)} %pack.1), channel_id=1, source_target_pairs={{0,64},{64,0},{1,65},{65,1},{2,66},{66,2},{3,67},{67,3},{4,68},{68... | collective-permute-start | bytes 1351688 | tf_op jit(solution)/shard_map/ppermute | solution.py:298
  23.8 14.2 %copy-start.12 = (f32[8,2]{0,1:T(2,128)S(1)}, f32[8,2]{0,1:T(2,128)}, u32[]{:S(2)}) copy-start(f32[8,2]{0,1:T(2,128)} %param.13) | copy-start | bytes 196
  34.0 15.1 %collective-permute-start.1 = (f32[2,2560]{1,0:T(2,128)S(1)}, f32[2,2560]{1,0:T(2,128)S(1)}, u32[]{:S(2)}, u32[]{:S(2)}) collective-permute-start(f32[2,2560]{1,0:T(2,128)S(1)} %add_convert_fusion), channel_id=1, source_target_pairs={{0,64},{64,0},{1,65},{65,1},{2,66},{66,2},{3,67},{67,3},{4,68},{68... | collective-permute-start | bytes 61448 | tf_op jit(solution)/shard_map/ppermute | solution.py:298
  37.7 11.7 %collective-permute-start = (bf16[80,2560]{1,0:T(8,128)(2,1)S(1)}, bf16[80,2560]{1,0:T(8,128)(2,1)S(1)}, u32[]{:S(2)}, u32[]{:S(2)}) collective-permute-start(bf16[80,2560]{1,0:T(8,128)(2,1)S(1)} %constant_dynamic-slice_fusion.2), channel_id=1, source_target_pairs={{0,64},{64,0},{1,65},{65,1},{2,66},{66,2},{3,67},{67,3},{4,68},{68... | collective-permute-start | bytes 1228808 | tf_op jit(solution)/shard_map/ppermute | solution.py:298
  178.5 0.9 copy-start.1
  179.4 0.9 copy-start.5
  180.3 20.5 %all-to-all-start.1 = ((bf16[32,112,128]{2,1,0:T(8,128)(2,1)}), bf16[32,112,128]{2,1,0:T(8,128)(2,1)S(1)}, u32[]{:S(2)}, u32[]{:S(2)}) async-start(bf16[32,112,128]{2,1,0:T(8,128)(2,1)} %copy-done.1), calls=%async_computation.1 | async-start | bytes 1835008 | tf_op jit(solution)/shard_map/all_to_all | solution.py:373
  200.9 1.1 copy-start.6
  215.6 1.1 copy-start
  216.7 0.9 copy-start.2
  217.6 0.8 copy-start.7
  218.3 28.0 %copy-start.3 = (f32[80,2560]{1,0:T(8,128)S(1)}, f32[80,2560]{1,0:T(8,128)}, u32[]{:S(2)}) copy-start(f32[80,2560]{1,0:T(8,128)} %copy-done.2) | copy-start | bytes 2457604
  218.3 27.9 %all-to-all-start.2 = ((bf16[32,160,128]{2,1,0:T(8,128)(2,1)}), bf16[32,160,128]{2,1,0:T(8,128)(2,1)S(1)}, u32[]{:S(2)}, u32[]{:S(2)}) async-start(bf16[32,160,128]{2,1,0:T(8,128)(2,1)} %bitcast.25), calls=%async_computation.2 | async-start | bytes 2621440 | tf_op jit(solution)/shard_map/all_to_all | solution.py:407
  222.4 23.9 %collective-permute-start.3 = (bf16[80,2560]{1,0:T(8,128)(2,1)}, bf16[80,2560]{1,0:T(8,128)(2,1)S(1)}, u32[]{:S(2)}, u32[]{:S(2)}) collective-permute-start(bf16[80,2560]{1,0:T(8,128)(2,1)} %copy-done.7), channel_id=1, source_target_pairs={{0,64},{64,0},{1,65},{65,1},{2,66},{66,2},{3,67},{67,3},{4,68},{68... | collective-permute-start | bytes 1228808 | tf_op jit(solution)/shard_map/ppermute | solution.py:298
Sparse Core Ops, SparseCore 0:
  23.9 101.8 all-gather.2

commit v4 on v3

--- a/solution.py
+++ b/solution.py
@@ -72,52 +72,60 @@
 
 def product(got_ref, mixed, total, held, sems, tiles):
     pairs = tiles // 2
-    blocks = got_ref.shape[0]
-    per_chunk = blocks // 2
-
-    def step(index, carry):
-        which = index // pairs
-        pair = lax.rem(index, pairs)
-
-        @pl.when(lax.rem(index, pairs // 2) == 0)
+    per_chunk = got_ref.shape[0] // 2
+
+    def step(pair, carry):
+        @pl.when(lax.rem(pair, pairs // 2) == 0)
         def _():
-            chunk = lax.rem(index // (pairs // 2), 2)
-
-            @pl.loop(0, per_chunk)
-            def _(k):
-                block_copy(got_ref, held, sems, which, chunk * per_chunk + k).wait()
+            chunk = pair // (pairs // 2)
+            for which in range(2):
+
+                @pl.loop(0, per_chunk)
+                def _(k):
+                    block_copy(got_ref, held, sems, which, chunk * per_chunk + k).wait()
 
         even = pl.multiple_of(pair * 2 * LANES, 2 * LANES)
         odd = pl.multiple_of(even + LANES, LANES)
 
-        def rows(start, low, high):
+        def rows(which, start, low, high):
             return held[which, pl.ds(start, LANES), low * LANES : high * LANES]
 
         def left(apart, count):
-            at = pl.multiple_of(even + apart * LANES, LANES)
-            return mixed[which, :, pl.ds(at, count * LANES)]
+            at = pl.ds(pl.multiple_of(even + apart * LANES, LANES), count * LANES)
+            return jnp.concatenate([mixed[0, :, at], mixed[1, :, at]], 1)
 
         def add(apart, count, value):
             at = pl.multiple_of(even + apart * LANES, LANES)
             total[:, pl.ds(at, count * LANES)] += value
 
-        def straight(a, w):
+        def straight(a, parts):
+            w = jnp.concatenate(parts, 0)
             return jnp.dot(a, w, preferred_element_type=F32)
 
-        def turned(a, w):
+        def turned(a, parts):
+            w = jnp.concatenate(parts, 1)
             return lax.dot_general(a, w, (((1,), (1,)), ((), ())), preferred_element_type=F32)
 
+        def two(start, low, high):
+            return [rows(w, start, low, high) for w in range(2)]
+
         span = pairs
-        both = jnp.concatenate([rows(even, 1, span + 1), rows(odd, 0, span)], 0)
-        add(1, span, straight(left(0, 2), both))
-        both = jnp.concatenate([rows(even, 2, span), rows(odd, 1, span - 1)], 0)
-        add(0, 2, -turned(left(2, span - 2), both))
-        add(0, 1, straight(left(0, 1), rows(even, 0, 1)) - turned(left(1, 1), rows(even, 1, 2)))
-        add(1, 1, -turned(left(span, 1), rows(odd, span - 1, span)))
-        add(span + 1, 1, straight(left(1, 1), rows(odd, span, span + 1)))
+        parts = []
+        for w in range(2):
+            parts += [rows(w, even, 1, span + 1), rows(w, odd, 0, span)]
+        add(1, span, straight(left(0, 2), parts))
+        parts = [
+            jnp.concatenate([rows(w, even, 2, span), rows(w, odd, 1, span - 1)], 0)
+            for w in range(2)
+        ]
+        add(0, 2, -turned(left(2, span - 2), parts))
+        near = straight(left(0, 1), two(even, 0, 1))
+        add(0, 1, near - turned(left(1, 1), two(even, 1, 2)))
+        add(1, 1, -turned(left(span, 1), two(odd, span - 1, span)))
+        add(span + 1, 1, straight(left(1, 1), two(odd, span, span + 1)))
         return carry
 
-    lax.fori_loop(0, 2 * pairs, step, 0)
+    lax.fori_loop(0, pairs, step, 0)
 
 
 def block_copy(got_ref, held, sems, which, block):
@@ -177,10 +185,7 @@
         back = shifted(back, begin + kept - rest * (s % group))
         return jnp.where(lane_index() >= begin + kept, back, front)
 
-    def far_safe(s, begin):
-        return far(s, begin)
-
-    return laid_out(near, half, tile), laid_out(far_safe, half, tile)
+    return laid_out(near, half, tile), laid_out(far, half, tile)
 
 
 def turn_rest(got_ref, turned, half):
@@ -243,7 +248,7 @@
 
 def last_kernel(
     half, tiles, scale, last_scale, first_ref, c_ref, back_ref, run_ref, own_ref, far_ref, got_ref,
-    leave, stay, columns, mixed, total, held, sems, turned, run,
+    leave, stay, columns, mixed, total, held, sems, turned, run, turned_all,
 ):
     begin(got_ref, held, sems)
 
@@ -260,17 +265,33 @@
         value = folded(total, tile, tiles).astype(F32)
         for channel in range(2):
             block = jnp.concatenate([value[channel * half : (channel + 1) * half], filler])
-            columns[channel, at, :] = block.T.astype(BF)
+            turned_all[channel, at, :] = block.T
         both = run[:, at] + value * last_scale
         leave[:, at] = jnp.where(first, both[half:], both[:half]).astype(BF)
         stay[:, at] = jnp.where(first, both[:half], both[half:])
+    tall, spare = 2 * half, LANES - half
+    high = columns.shape[2]
+    for channel in range(2):
+        for row in range(columns.shape[1]):
+            base = turned_all[channel, row * tall : row * tall + high]
+            tail = turned_all[channel, row * tall + high : (row + 1) * tall]
+            side = jnp.concatenate([shifted(tail, half), shifted(tail, half - spare)])
+            side = jnp.concatenate([side, jnp.zeros((high - side.shape[0], LANES), F32)])
+            columns[channel, row] = jnp.where(lane_index() < half, base, side).astype(BF)
 
 
 def end_kernel(half, scale, first_ref, ham_ref, stay_ref, land_ref, got_ref, out_ref):
     first = first_ref[0] != 0
 
+    spare = LANES - half
+    left_over = 2 * half - got_ref.shape[2]
+
     def piece(s, begin):
-        return shifted(got_ref[s % 2, s // 2].astype(F32), begin)
+        block = got_ref[s % 2, s // 2].astype(F32)
+        front = shifted(block[:left_over], begin - half)
+        back = shifted(block[left_over : 2 * left_over], begin - half + spare)
+        tail = jnp.where(lane_index() >= begin + spare, back, front)
+        return jnp.concatenate([shifted(block, begin), tail])
 
     for tile in range(ham_ref.shape[1] // LANES):
         at = slice(tile * LANES, (tile + 1) * LANES)
@@ -396,16 +417,18 @@
         [
             shape((half, state_count), BF),
             shape((half, state_count), F32),
-            shape((2, state_count, LANES), BF),
+            shape((2, shard_count, half + rest, LANES), BF),
         ],
         [SMEM] + [VMEM] * 5 + [HBM],
         "last",
-        scratch + more + [pltpu.VMEM((row_count, state_count), F32)],
+        scratch
+        + more
+        + [pltpu.VMEM((row_count, state_count), F32), pltpu.VMEM((2, state_count, LANES), F32)],
         cost,
     )(which, combined, back, running, own_set, far_set, gathered)
     landed = swapped(leaving)
     got = lax.all_to_all(
-        blocks.reshape(destinations, row_count, LANES),
+        blocks.reshape(destinations, half + rest, LANES),
         ("hi", "row"),
         split_axis=0,
         concat_axis=0,
@@ -416,7 +439,7 @@
         shape((row_count, state_count), F32),
         [SMEM] + [VMEM] * 4,
         "finish",
-    )(which, own_ham, staying, landed, got.reshape(2, shard_count, row_count, LANES))
+    )(which, own_ham, staying, landed, got.reshape(2, shard_count, half + rest, LANES))
     return result[None]
 
 

time: 256 us -> 251 us (0.980)
  waiting for transfers between devices: 124 us -> 120 us
    ppermute x4, waiting for transfers between devices: 30.9 us -> 27 us  [swapped(): return lax.ppermute(value, 'hi', [(0, 1), (1, 0)])]
    unnamed x26 -> x28, local copies, waits for them, and re-layouts: 6.85 us -> 6.73 us
  transfers between devices with their start and end apart: 7 -> 7, of which waited for: 5 -> 5; matrix products, arithmetic and copies ran while one was open for 4% -> 5% of each run, Pallas kernels for 0% -> 0%
where the time goes in v4:
time: 251 us; the launch traced here: 250 us
  waiting for transfers between devices  120 us (48%)
  Pallas kernels  42.9 us (17%)
  blocking collectives  25.6 us (10%)
  between operations  24.3 us (10%)
  starting transfers between devices  18.2 us (7%)
  local copies, waits for them, and re-layouts  17.4 us (7%)
    all_gather x1, waiting for transfers between devices, on_device(): gathered = lax.all_gather(both, 'row', axis=0, tiled=False)  76.3 us
    ppermute x4, waiting for transfers between devices, swapped(): return lax.ppermute(value, 'hi', [(0, 1), (1, 0)])  27 us
    all_to_all x1, blocking collectives, exchanged(): lax.all_to_all(columns, ('row', 'hi'), split_axis=0, concat_axis=0, tiled...  25.6 us
    all_to_all x1, waiting for transfers between devices, exchanged(): lax.all_to_all(columns, ('row', 'hi'), split_axis=0, concat_axis=0, tiled...  16.6 us
    pallas_call x1, Pallas kernels, on_device(): call(functools.partial(last_kernel, half, tiles, -0.5, -1.0 / TERMS), [sh...  13.6 us
    pallas_call x1, Pallas kernels, on_device(): call(functools.partial(middle_kernel, half, tiles, -1.0), [c_shape, run_s...  13.3 us
    pallas_call x1, Pallas kernels, on_device(): call(functools.partial(first_kernel, half, tiles), [c_shape, sent_shape],...  13.3 us
    ppermute x4, starting transfers between devices, swapped(): return lax.ppermute(value, 'hi', [(0, 1), (1, 0)])  10.3 us
  transfers between devices with their start and end apart: 7, of which 5 were waited for; matrix products, arithmetic and copies ran while one was open for 5% of the time, Pallas kernels for 0%

profile of v4, /device:TPU:0, one launch (start us, length us, event | category | flops | bytes accessed | tf_op | source)
XLA Modules:
  0.0 250.3 jit_solution(1241728547650021565)
XLA Ops:
  7.3 1.1 copy-done.4
  8.4 0.8 pack.1
  9.2 3.2 %collective-permute-start.2 = (bf16[160,1408]{1,0:T(8,128)(2,1)S(1)}, bf16[160,1408]{1,0:T(8,128)(2,1)S(1)}, u32[]{:S(2)}, u32[]{:S(2)}) collective-permute-start(bf16[160,1408]{1,0:T(8,128)(2,1)S(1)} %pack.1), channel_id=1, source_target_pairs={{0,64},{64,0},{1,65},{65,1},{2,66},{66,2},{3,67},{67,3},{4,68},{68... | collective-permute-start | bytes 1351688 | tf_op jit(solution)/shard_map/ppermute | solution.py:319
  12.4 10.3 %collective-permute-done.2 = bf16[160,1408]{1,0:T(8,128)(2,1)S(1)} collective-permute-done((bf16[160,1408]{1,0:T(8,128)(2,1)S(1)}, bf16[160,1408]{1,0:T(8,128)(2,1)S(1)}, u32[]{:S(2)}, u32[]{:S(2)}) %collective-permute-start.2) | collective-permute-done | bytes 450592 | tf_op jit(solution)/shard_map/ppermute | solution.py:319
  22.8 1.0 pad_maximum_fusion
  23.9 9.9 %scatter_custom_fusion = s32[2560]{0:T(1024)S(1)} fusion(s32[2560]{0:T(1024)S(1)} %fusion, s32[2560]{0:T(1024)S(1)} %reduce.1, s32[]{:T(128)} %constant.8.clone.1), kind=kCustom, calls=%fused_computation.24 | custom fusion | bytes 10244 | tf_op jit(solution)/shard_map/scatter | solution.py:353
  34.0 3.3 %collective-permute-start.1 = (f32[2,2560]{1,0:T(2,128)S(1)}, f32[2,2560]{1,0:T(2,128)S(1)}, u32[]{:S(2)}, u32[]{:S(2)}) collective-permute-start(f32[2,2560]{1,0:T(2,128)S(1)} %add_convert_fusion), channel_id=1, source_target_pairs={{0,64},{64,0},{1,65},{65,1},{2,66},{66,2},{3,67},{67,3},{4,68},{68... | collective-permute-start | bytes 61448 | tf_op jit(solution)/shard_map/ppermute | solution.py:319
  49.5 76.3 %all-gather.3.cloned.1.call-done = bf16[32,160,1408]{2,1,0:T(8,128)(2,1)} async-done(((bf16[2,160,1408]{2,1,0:T(8,128)(2,1)}), bf16[32,160,1408]{2,1,0:T(8,128)(2,1)}) %all-gather.3.cloned.1.call-update) | async-done | bytes 14417936 | tf_op jit(solution)/shard_map/all_gather | solution.py:351
  125.9 13.3 %first.1 = (bf16[160,2560]{1,0:T(8,128)(2,1)S(1)}, bf16[32,112,128]{2,1,0:T(8,128)(2,1)S(1)}) custom-call(bf16[160,2560]{1,0:T(8,128)(2,1)S(1)} %pad_maximum_fusion.1.x_ref, f32[4,2560]{1,0:T(4,128)S(1)} %get-tuple-element.24.own_ref, f32[4,2560]{1,0:T(4,128)S(1)} %get-tuple-element.23.far_ref, bf16[16,2,160,1408]{3,2,1,0:T(8,128)(2,1)} %bitcast.27), custom_call_target="tpu_custom_call" | custom-call | flops 4194304000 | bytes 14417920 | tf_op jit(solution)/shard_map/first/pallas_call | solution.py:396
  139.2 25.6 %all_to_all.15.back_ref = bf16[32,112,128]{2,1,0:T(8,128)(2,1)S(1)} all-to-all(bf16[32,112,128]{2,1,0:T(8,128)(2,1)S(1)} %get-tuple-element.14), channel_id=1, replica_groups=mesh['hi'=2,'lo'=4,'row'=16] {'row','hi'}, dimensions={0} | all-to-all | bytes 1835008 | tf_op jit(solution)/shard_map/all_to_all | solution.py:394
  164.7 13.3 %middle.1 = (bf16[160,2560]{1,0:T(8,128)(2,1)S(1)}, f32[160,2560]{1,0:T(8,128)S(1)}, bf16[32,112,128]{2,1,0:T(8,128)(2,1)S(1)}) custom-call(bf16[160,2560]{1,0:T(8,128)(2,1)S(1)} %get-tuple-element.13.c_ref, bf16[32,112,128]{2,1,0:T(8,128)(2,1)S(1)} %all_to_all.15.back_ref, f32[4,2560]{1,0:T(4,128)S(1)} %get-tuple-element.24.own_ref, ...), custom_call_target="tpu_custom_call" | custom-call | flops 4194304000 | bytes 14417920 | tf_op jit(solution)/shard_map/middle/pallas_call | solution.py:405
  178.1 0.9 copy-done.1
  179.0 0.9 copy-done.5
  179.9 3.9 %all-to-all-start.1 = ((bf16[32,112,128]{2,1,0:T(8,128)(2,1)}), bf16[32,112,128]{2,1,0:T(8,128)(2,1)S(1)}, u32[]{:S(2)}, u32[]{:S(2)}) async-start(bf16[32,112,128]{2,1,0:T(8,128)(2,1)} %copy-done.1), calls=%async_computation.1 | async-start | bytes 1835008 | tf_op jit(solution)/shard_map/all_to_all | solution.py:394
  183.8 16.6 %all-to-all-done.1.back_ref = bf16[32,112,128]{2,1,0:T(8,128)(2,1)S(1)} async-done(((bf16[32,112,128]{2,1,0:T(8,128)(2,1)}), bf16[32,112,128]{2,1,0:T(8,128)(2,1)S(1)}, u32[]{:S(2)}, u32[]{:S(2)}) %all-to-all-start.1) | async-done | bytes 917536 | tf_op jit(solution)/shard_map/all_to_all | solution.py:394
  200.5 1.1 copy-done.6
  201.6 13.6 %last.1 = (bf16[80,2560]{1,0:T(8,128)(2,1)S(1)}, f32[80,2560]{1,0:T(8,128)S(1)}, bf16[2,16,112,128]{3,2,1,0:T(8,128)(2,1)S(1)}) custom-call(s32[1]{0:T(128)} %bitcast.first_ref, bf16[160,2560]{1,0:T(8,128)(2,1)S(1)} %copy-done.6, bf16[32,112,128]{2,1,0:T(8,128)(2,1)S(1)} %all-to-all-done.1.back_ref, f32[160,2560]{1,0:T(8,128)S(1)} %get-tuple-element.17.run_ref, ...), custom_call_target="tpu_custom_call" | custom-call | flops 4194304000 | bytes 14417920 | tf_op jit(solution)/shard_map/last/pallas_call | solution.py:415
  215.2 0.9 copy-done
  216.1 0.9 copy-done.2
  217.1 0.8 copy-done.7
  217.8 4.1 %all-to-all-start.2 = ((bf16[32,112,128]{2,1,0:T(8,128)(2,1)}), bf16[32,112,128]{2,1,0:T(8,128)(2,1)S(1)}, u32[]{:S(2)}, u32[]{:S(2)}) async-start(bf16[32,112,128]{2,1,0:T(8,128)(2,1)} %bitcast.25), calls=%async_computation.2 | async-start | bytes 1835008 | tf_op jit(solution)/shard_map/all_to_all | solution.py:430
  221.9 3.4 %collective-permute-start.3 = (bf16[80,2560]{1,0:T(8,128)(2,1)S(1)}, bf16[80,2560]{1,0:T(8,128)(2,1)S(1)}, u32[]{:S(2)}, u32[]{:S(2)}) collective-permute-start(bf16[80,2560]{1,0:T(8,128)(2,1)S(1)} %copy-done.8), channel_id=1, source_target_pairs={{0,64},{64,0},{1,65},{65,1},{2,66},{66,2},{3,67},{67,3},{4,68},{68... | collective-permute-start | bytes 1228808 | tf_op jit(solution)/shard_map/ppermute | solution.py:319
  225.3 16.3 %collective-permute-done.3.land_ref = bf16[80,2560]{1,0:T(8,128)(2,1)S(1)} collective-permute-done((bf16[80,2560]{1,0:T(8,128)(2,1)S(1)}, bf16[80,2560]{1,0:T(8,128)(2,1)S(1)}, u32[]{:S(2)}, u32[]{:S(2)}) %collective-permute-start.3) | collective-permute-done | bytes 409632 | tf_op jit(solution)/shard_map/ppermute | solution.py:319
  241.6 1.9 finish.1
  (45 shorter events, 2.4 us)
Async XLA Ops:
  6.5 119.3 %all-gather.3.cloned.1.call-start = ((), (), s32[]{:S(2)}) async-start(), calls=%async_computation.3 | async-start | bytes 15319040 | tf_op jit(solution)/shard_map/all_gather | solution.py:351
  7.3 1.1 copy-start.4
  9.2 14.6 %copy-start.10 = (s32[1,2560]{1,0:T(1,128)S(1)}, s32[1,2560]{1,0:T(1,128)}, u32[]{:S(2)}) copy-start(s32[1,2560]{1,0:T(1,128)} %param.11) | copy-start | bytes 30724
  9.2 14.7 %copy-start.11 = (s32[1,2560]{1,0:T(1,128)S(1)}, s32[1,2560]{1,0:T(1,128)}, u32[]{:S(2)}) copy-start(s32[1,2560]{1,0:T(1,128)} %param.12) | copy-start | bytes 30724
  9.2 24.7 %copy-start.12 = (s32[1,2560]{1,0:T(1,128)S(1)}, s32[1,2560]{1,0:T(1,128)}, u32[]{:S(2)}) copy-start(s32[1,2560]{1,0:T(1,128)} %param.10) | copy-start | bytes 30724
  9.2 28.1 %copy-start.9 = (bf16[1,160,2560]{2,1,0:T(8,128)(2,1)S(1)}, bf16[1,160,2560]{2,1,0:T(8,128)(2,1)}, u32[]{:S(2)}) copy-start(bf16[1,160,2560]{2,1,0:T(8,128)(2,1)} %param.8) | copy-start | bytes 2457604
  9.2 13.6 %collective-permute-start.2 = (bf16[160,1408]{1,0:T(8,128)(2,1)S(1)}, bf16[160,1408]{1,0:T(8,128)(2,1)S(1)}, u32[]{:S(2)}, u32[]{:S(2)}) collective-permute-start(bf16[160,1408]{1,0:T(8,128)(2,1)S(1)} %pack.1), channel_id=1, source_target_pairs={{0,64},{64,0},{1,65},{65,1},{2,66},{66,2},{3,67},{67,3},{4,68},{68... | collective-permute-start | bytes 1351688 | tf_op jit(solution)/shard_map/ppermute | solution.py:319
  23.8 14.2 %copy-start.13 = (f32[8,2]{0,1:T(2,128)S(1)}, f32[8,2]{0,1:T(2,128)}, u32[]{:S(2)}) copy-start(f32[8,2]{0,1:T(2,128)} %param.13) | copy-start | bytes 196
  34.0 14.8 %collective-permute-start.1 = (f32[2,2560]{1,0:T(2,128)S(1)}, f32[2,2560]{1,0:T(2,128)S(1)}, u32[]{:S(2)}, u32[]{:S(2)}) collective-permute-start(f32[2,2560]{1,0:T(2,128)S(1)} %add_convert_fusion), channel_id=1, source_target_pairs={{0,64},{64,0},{1,65},{65,1},{2,66},{66,2},{3,67},{67,3},{4,68},{68... | collective-permute-start | bytes 61448 | tf_op jit(solution)/shard_map/ppermute | solution.py:319
  37.7 11.7 %collective-permute-start = (bf16[80,2560]{1,0:T(8,128)(2,1)S(1)}, bf16[80,2560]{1,0:T(8,128)(2,1)S(1)}, u32[]{:S(2)}, u32[]{:S(2)}) collective-permute-start(bf16[80,2560]{1,0:T(8,128)(2,1)S(1)} %constant_dynamic-slice_fusion.2), channel_id=1, source_target_pairs={{0,64},{64,0},{1,65},{65,1},{2,66},{66,2},{3,67},{67,3},{4,68},{68... | collective-permute-start | bytes 1228808 | tf_op jit(solution)/shard_map/ppermute | solution.py:319
  178.1 0.9 copy-start.1
  179.0 0.9 copy-start.5
  179.9 20.6 %all-to-all-start.1 = ((bf16[32,112,128]{2,1,0:T(8,128)(2,1)}), bf16[32,112,128]{2,1,0:T(8,128)(2,1)S(1)}, u32[]{:S(2)}, u32[]{:S(2)}) async-start(bf16[32,112,128]{2,1,0:T(8,128)(2,1)} %copy-done.1), calls=%async_computation.1 | async-start | bytes 1835008 | tf_op jit(solution)/shard_map/all_to_all | solution.py:394
  200.5 1.1 copy-start.6
  215.2 0.9 copy-start
  216.1 0.9 copy-start.2
  217.0 0.8 copy-start.7
  217.8 4.1 %copy-start.8 = (bf16[80,2560]{1,0:T(8,128)(2,1)S(1)}, bf16[80,2560]{1,0:T(8,128)(2,1)}, u32[]{:S(2)}) copy-start(bf16[80,2560]{1,0:T(8,128)(2,1)} %copy-done.7) | copy-start | bytes 1228804
  217.8 23.7 %copy-start.3 = (f32[80,2560]{1,0:T(8,128)S(1)}, f32[80,2560]{1,0:T(8,128)}, u32[]{:S(2)}) copy-start(f32[80,2560]{1,0:T(8,128)} %copy-done.2) | copy-start | bytes 2457604
  217.8 23.7 %all-to-all-start.2 = ((bf16[32,112,128]{2,1,0:T(8,128)(2,1)}), bf16[32,112,128]{2,1,0:T(8,128)(2,1)S(1)}, u32[]{:S(2)}, u32[]{:S(2)}) async-start(bf16[32,112,128]{2,1,0:T(8,128)(2,1)} %bitcast.25), calls=%async_computation.2 | async-start | bytes 1835008 | tf_op jit(solution)/shard_map/all_to_all | solution.py:430
  221.9 19.7 %collective-permute-start.3 = (bf16[80,2560]{1,0:T(8,128)(2,1)S(1)}, bf16[80,2560]{1,0:T(8,128)(2,1)S(1)}, u32[]{:S(2)}, u32[]{:S(2)}) collective-permute-start(bf16[80,2560]{1,0:T(8,128)(2,1)S(1)} %copy-done.8), channel_id=1, source_target_pairs={{0,64},{64,0},{1,65},{65,1},{2,66},{66,2},{3,67},{67,3},{4,68},{68... | collective-permute-start | bytes 1228808 | tf_op jit(solution)/shard_map/ppermute | solution.py:319
Sparse Core Ops, SparseCore 0:
  23.9 101.8 all-gather.2

commit v5 on v4

--- a/solution.py
+++ b/solution.py
@@ -72,17 +72,17 @@
 
 def product(got_ref, mixed, total, held, sems, tiles):
     pairs = tiles // 2
-    per_chunk = got_ref.shape[0] // 2
 
     def step(pair, carry):
-        @pl.when(lax.rem(pair, pairs // 2) == 0)
-        def _():
-            chunk = pair // (pairs // 2)
+        rows_of = got_ref.shape[2]
+
+        def blocks_before(p):
+            return (p * 2 * LANES + rows_of - 1) // rows_of
+
+        @pl.loop(blocks_before(pair), blocks_before(pair + 1))
+        def _(block):
             for which in range(2):
-
-                @pl.loop(0, per_chunk)
-                def _(k):
-                    block_copy(got_ref, held, sems, which, chunk * per_chunk + k).wait()
+                block_copy(got_ref, held, sems, which, block).wait()
 
         even = pl.multiple_of(pair * 2 * LANES, 2 * LANES)
         odd = pl.multiple_of(even + LANES, LANES)
@@ -137,10 +137,9 @@
 
 
 def begin(got_ref, held, sems):
-    for which in range(2):
-
-        @pl.loop(0, got_ref.shape[0])
-        def _(block):
+    @pl.loop(0, got_ref.shape[0])
+    def _(block):
+        for which in range(2):
             block_copy(got_ref, held, sems, which, block).start()
 
 

time: 251 us -> 243 us (0.968)
  Pallas kernels: 42.9 us -> 35.1 us
    pallas_call x1, Pallas kernels: 13.3 us -> 10.6 us  [on_device(): call(functools.partial(first_kernel, half, tiles), [c_shape, sent_shape],...]
    pallas_call x1, Pallas kernels: 13.3 us -> 10.7 us  [on_device(): call(functools.partial(middle_kernel, half, tiles, -1.0), [c_shape, run_s...]
    pallas_call x1, Pallas kernels: 13.6 us -> 11.1 us  [on_device(): call(functools.partial(last_kernel, half, tiles, -0.5, -1.0 / TERMS), [sh...]
where the time goes in v5:
time: 243 us; the launch traced here: 242 us
  waiting for transfers between devices  120 us (49%)
  Pallas kernels  35.1 us (14%)
  blocking collectives  25.6 us (11%)
  between operations  24.3 us (10%)
  starting transfers between devices  18.2 us (7%)
  local copies, waits for them, and re-layouts  17.4 us (7%)
    all_gather x1, waiting for transfers between devices, on_device(): gathered = lax.all_gather(both, 'row', axis=0, tiled=False)  76.3 us
    ppermute x4, waiting for transfers between devices, swapped(): return lax.ppermute(value, 'hi', [(0, 1), (1, 0)])  27 us
    all_to_all x1, blocking collectives, exchanged(): lax.all_to_all(columns, ('row', 'hi'), split_axis=0, concat_axis=0, tiled...  25.6 us
    all_to_all x1, waiting for transfers between devices, exchanged(): lax.all_to_all(columns, ('row', 'hi'), split_axis=0, concat_axis=0, tiled...  16.6 us
    pallas_call x1, Pallas kernels, on_device(): call(functools.partial(last_kernel, half, tiles, -0.5, -1.0 / TERMS), [sh...  11.1 us
    pallas_call x1, Pallas kernels, on_device(): call(functools.partial(middle_kernel, half, tiles, -1.0), [c_shape, run_s...  10.7 us
    pallas_call x1, Pallas kernels, on_device(): call(functools.partial(first_kernel, half, tiles), [c_shape, sent_shape],...  10.6 us
    ppermute x4, starting transfers between devices, swapped(): return lax.ppermute(value, 'hi', [(0, 1), (1, 0)])  10.3 us
  transfers between devices with their start and end apart: 7, of which 5 were waited for; matrix products, arithmetic and copies ran while one was open for 5% of the time, Pallas kernels for 0%

profile of v5, /device:TPU:0, one launch (start us, length us, event | category | flops | bytes accessed | tf_op | source)
XLA Modules:
  0.0 242.4 jit_solution(1388338365683931648)
XLA Ops:
  7.3 1.1 copy-done.4
  8.4 0.8 pack.1
  9.2 3.2 %collective-permute-start.2 = (bf16[160,1408]{1,0:T(8,128)(2,1)S(1)}, bf16[160,1408]{1,0:T(8,128)(2,1)S(1)}, u32[]{:S(2)}, u32[]{:S(2)}) collective-permute-start(bf16[160,1408]{1,0:T(8,128)(2,1)S(1)} %pack.1), channel_id=1, source_target_pairs={{0,64},{64,0},{1,65},{65,1},{2,66},{66,2},{3,67},{67,3},{4,68},{68... | collective-permute-start | bytes 1351688 | tf_op jit(solution)/shard_map/ppermute | solution.py:318
  12.4 10.3 %collective-permute-done.2 = bf16[160,1408]{1,0:T(8,128)(2,1)S(1)} collective-permute-done((bf16[160,1408]{1,0:T(8,128)(2,1)S(1)}, bf16[160,1408]{1,0:T(8,128)(2,1)S(1)}, u32[]{:S(2)}, u32[]{:S(2)}) %collective-permute-start.2) | collective-permute-done | bytes 450592 | tf_op jit(solution)/shard_map/ppermute | solution.py:318
  22.8 1.0 pad_maximum_fusion
  23.9 9.9 %scatter_custom_fusion = s32[2560]{0:T(1024)S(1)} fusion(s32[2560]{0:T(1024)S(1)} %fusion, s32[2560]{0:T(1024)S(1)} %reduce.1, s32[]{:T(128)} %constant.8.clone.1), kind=kCustom, calls=%fused_computation.24 | custom fusion | bytes 10244 | tf_op jit(solution)/shard_map/scatter | solution.py:352
  34.0 3.3 %collective-permute-start.1 = (f32[2,2560]{1,0:T(2,128)S(1)}, f32[2,2560]{1,0:T(2,128)S(1)}, u32[]{:S(2)}, u32[]{:S(2)}) collective-permute-start(f32[2,2560]{1,0:T(2,128)S(1)} %add_convert_fusion), channel_id=1, source_target_pairs={{0,64},{64,0},{1,65},{65,1},{2,66},{66,2},{3,67},{67,3},{4,68},{68... | collective-permute-start | bytes 61448 | tf_op jit(solution)/shard_map/ppermute | solution.py:318
  49.5 76.3 %all-gather.3.cloned.1.call-done = bf16[32,160,1408]{2,1,0:T(8,128)(2,1)} async-done(((bf16[2,160,1408]{2,1,0:T(8,128)(2,1)}), bf16[32,160,1408]{2,1,0:T(8,128)(2,1)}) %all-gather.3.cloned.1.call-update) | async-done | bytes 14417936 | tf_op jit(solution)/shard_map/all_gather | solution.py:350
  125.9 10.6 %first.1 = (bf16[160,2560]{1,0:T(8,128)(2,1)S(1)}, bf16[32,112,128]{2,1,0:T(8,128)(2,1)S(1)}) custom-call(bf16[160,2560]{1,0:T(8,128)(2,1)S(1)} %pad_maximum_fusion.1.x_ref, f32[4,2560]{1,0:T(4,128)S(1)} %get-tuple-element.24.own_ref, f32[4,2560]{1,0:T(4,128)S(1)} %get-tuple-element.23.far_ref, bf16[16,2,160,1408]{3,2,1,0:T(8,128)(2,1)} %bitcast.27), custom_call_target="tpu_custom_call" | custom-call | flops 4194304000 | bytes 14417920 | tf_op jit(solution)/shard_map/first/pallas_call | solution.py:395
  136.5 25.6 %all_to_all.15.back_ref = bf16[32,112,128]{2,1,0:T(8,128)(2,1)S(1)} all-to-all(bf16[32,112,128]{2,1,0:T(8,128)(2,1)S(1)} %get-tuple-element.14), channel_id=1, replica_groups=mesh['hi'=2,'lo'=4,'row'=16] {'row','hi'}, dimensions={0} | all-to-all | bytes 1835008 | tf_op jit(solution)/shard_map/all_to_all | solution.py:393
  162.1 10.7 %middle.1 = (bf16[160,2560]{1,0:T(8,128)(2,1)S(1)}, f32[160,2560]{1,0:T(8,128)S(1)}, bf16[32,112,128]{2,1,0:T(8,128)(2,1)S(1)}) custom-call(bf16[160,2560]{1,0:T(8,128)(2,1)S(1)} %get-tuple-element.13.c_ref, bf16[32,112,128]{2,1,0:T(8,128)(2,1)S(1)} %all_to_all.15.back_ref, f32[4,2560]{1,0:T(4,128)S(1)} %get-tuple-element.24.own_ref, ...), custom_call_target="tpu_custom_call" | custom-call | flops 4194304000 | bytes 14417920 | tf_op jit(solution)/shard_map/middle/pallas_call | solution.py:404
  172.8 0.9 copy-done.1
  173.8 0.9 copy-done.5
  174.7 3.9 %all-to-all-start.1 = ((bf16[32,112,128]{2,1,0:T(8,128)(2,1)}), bf16[32,112,128]{2,1,0:T(8,128)(2,1)S(1)}, u32[]{:S(2)}, u32[]{:S(2)}) async-start(bf16[32,112,128]{2,1,0:T(8,128)(2,1)} %copy-done.1), calls=%async_computation.1 | async-start | bytes 1835008 | tf_op jit(solution)/shard_map/all_to_all | solution.py:393
  178.6 16.6 %all-to-all-done.1.back_ref = bf16[32,112,128]{2,1,0:T(8,128)(2,1)S(1)} async-done(((bf16[32,112,128]{2,1,0:T(8,128)(2,1)}), bf16[32,112,128]{2,1,0:T(8,128)(2,1)S(1)}, u32[]{:S(2)}, u32[]{:S(2)}) %all-to-all-start.1) | async-done | bytes 917536 | tf_op jit(solution)/shard_map/all_to_all | solution.py:393
  195.2 1.1 copy-done.6
  196.3 11.1 %last.1 = (bf16[80,2560]{1,0:T(8,128)(2,1)S(1)}, f32[80,2560]{1,0:T(8,128)S(1)}, bf16[2,16,112,128]{3,2,1,0:T(8,128)(2,1)S(1)}) custom-call(s32[1]{0:T(128)} %bitcast.first_ref, bf16[160,2560]{1,0:T(8,128)(2,1)S(1)} %copy-done.6, bf16[32,112,128]{2,1,0:T(8,128)(2,1)S(1)} %all-to-all-done.1.back_ref, f32[160,2560]{1,0:T(8,128)S(1)} %get-tuple-element.17.run_ref, ...), custom_call_target="tpu_custom_call" | custom-call | flops 4194304000 | bytes 14417920 | tf_op jit(solution)/shard_map/last/pallas_call | solution.py:414
  207.4 0.9 copy-done
  208.3 0.9 copy-done.2
  209.3 0.8 copy-done.7
  210.0 4.1 %all-to-all-start.2 = ((bf16[32,112,128]{2,1,0:T(8,128)(2,1)}), bf16[32,112,128]{2,1,0:T(8,128)(2,1)S(1)}, u32[]{:S(2)}, u32[]{:S(2)}) async-start(bf16[32,112,128]{2,1,0:T(8,128)(2,1)} %bitcast.25), calls=%async_computation.2 | async-start | bytes 1835008 | tf_op jit(solution)/shard_map/all_to_all | solution.py:429
  214.1 3.4 %collective-permute-start.3 = (bf16[80,2560]{1,0:T(8,128)(2,1)S(1)}, bf16[80,2560]{1,0:T(8,128)(2,1)S(1)}, u32[]{:S(2)}, u32[]{:S(2)}) collective-permute-start(bf16[80,2560]{1,0:T(8,128)(2,1)S(1)} %copy-done.8), channel_id=1, source_target_pairs={{0,64},{64,0},{1,65},{65,1},{2,66},{66,2},{3,67},{67,3},{4,68},{68... | collective-permute-start | bytes 1228808 | tf_op jit(solution)/shard_map/ppermute | solution.py:318
  217.5 16.3 %collective-permute-done.3.land_ref = bf16[80,2560]{1,0:T(8,128)(2,1)S(1)} collective-permute-done((bf16[80,2560]{1,0:T(8,128)(2,1)S(1)}, bf16[80,2560]{1,0:T(8,128)(2,1)S(1)}, u32[]{:S(2)}, u32[]{:S(2)}) %collective-permute-start.3) | collective-permute-done | bytes 409632 | tf_op jit(solution)/shard_map/ppermute | solution.py:318
  233.7 1.9 finish.1
  (45 shorter events, 2.4 us)
Async XLA Ops:
  6.5 119.3 %all-gather.3.cloned.1.call-start = ((), (), s32[]{:S(2)}) async-start(), calls=%async_computation.3 | async-start | bytes 15319040 | tf_op jit(solution)/shard_map/all_gather | solution.py:350
  7.3 1.1 copy-start.4
  9.2 14.6 %copy-start.10 = (s32[1,2560]{1,0:T(1,128)S(1)}, s32[1,2560]{1,0:T(1,128)}, u32[]{:S(2)}) copy-start(s32[1,2560]{1,0:T(1,128)} %param.11) | copy-start | bytes 30724
  9.2 14.7 %copy-start.11 = (s32[1,2560]{1,0:T(1,128)S(1)}, s32[1,2560]{1,0:T(1,128)}, u32[]{:S(2)}) copy-start(s32[1,2560]{1,0:T(1,128)} %param.12) | copy-start | bytes 30724
  9.2 24.7 %copy-start.12 = (s32[1,2560]{1,0:T(1,128)S(1)}, s32[1,2560]{1,0:T(1,128)}, u32[]{:S(2)}) copy-start(s32[1,2560]{1,0:T(1,128)} %param.10) | copy-start | bytes 30724
  9.2 28.1 %copy-start.9 = (bf16[1,160,2560]{2,1,0:T(8,128)(2,1)S(1)}, bf16[1,160,2560]{2,1,0:T(8,128)(2,1)}, u32[]{:S(2)}) copy-start(bf16[1,160,2560]{2,1,0:T(8,128)(2,1)} %param.8) | copy-start | bytes 2457604
  9.2 13.6 %collective-permute-start.2 = (bf16[160,1408]{1,0:T(8,128)(2,1)S(1)}, bf16[160,1408]{1,0:T(8,128)(2,1)S(1)}, u32[]{:S(2)}, u32[]{:S(2)}) collective-permute-start(bf16[160,1408]{1,0:T(8,128)(2,1)S(1)} %pack.1), channel_id=1, source_target_pairs={{0,64},{64,0},{1,65},{65,1},{2,66},{66,2},{3,67},{67,3},{4,68},{68... | collective-permute-start | bytes 1351688 | tf_op jit(solution)/shard_map/ppermute | solution.py:318
  23.8 14.2 %copy-start.13 = (f32[8,2]{0,1:T(2,128)S(1)}, f32[8,2]{0,1:T(2,128)}, u32[]{:S(2)}) copy-start(f32[8,2]{0,1:T(2,128)} %param.13) | copy-start | bytes 196
  34.0 14.8 %collective-permute-start.1 = (f32[2,2560]{1,0:T(2,128)S(1)}, f32[2,2560]{1,0:T(2,128)S(1)}, u32[]{:S(2)}, u32[]{:S(2)}) collective-permute-start(f32[2,2560]{1,0:T(2,128)S(1)} %add_convert_fusion), channel_id=1, source_target_pairs={{0,64},{64,0},{1,65},{65,1},{2,66},{66,2},{3,67},{67,3},{4,68},{68... | collective-permute-start | bytes 61448 | tf_op jit(solution)/shard_map/ppermute | solution.py:318
  37.7 11.7 %collective-permute-start = (bf16[80,2560]{1,0:T(8,128)(2,1)S(1)}, bf16[80,2560]{1,0:T(8,128)(2,1)S(1)}, u32[]{:S(2)}, u32[]{:S(2)}) collective-permute-start(bf16[80,2560]{1,0:T(8,128)(2,1)S(1)} %constant_dynamic-slice_fusion.2), channel_id=1, source_target_pairs={{0,64},{64,0},{1,65},{65,1},{2,66},{66,2},{3,67},{67,3},{4,68},{68... | collective-permute-start | bytes 1228808 | tf_op jit(solution)/shard_map/ppermute | solution.py:318
  172.8 0.9 copy-start.1
  173.8 0.9 copy-start.5
  174.7 20.5 %all-to-all-start.1 = ((bf16[32,112,128]{2,1,0:T(8,128)(2,1)}), bf16[32,112,128]{2,1,0:T(8,128)(2,1)S(1)}, u32[]{:S(2)}, u32[]{:S(2)}) async-start(bf16[32,112,128]{2,1,0:T(8,128)(2,1)} %copy-done.1), calls=%async_computation.1 | async-start | bytes 1835008 | tf_op jit(solution)/shard_map/all_to_all | solution.py:393
  195.2 1.1 copy-start.6
  207.4 0.9 copy-start
  208.3 0.9 copy-start.2
  209.3 0.8 copy-start.7
  210.0 4.1 %copy-start.8 = (bf16[80,2560]{1,0:T(8,128)(2,1)S(1)}, bf16[80,2560]{1,0:T(8,128)(2,1)}, u32[]{:S(2)}) copy-start(bf16[80,2560]{1,0:T(8,128)(2,1)} %copy-done.7) | copy-start | bytes 1228804
  210.0 23.7 %copy-start.3 = (f32[80,2560]{1,0:T(8,128)S(1)}, f32[80,2560]{1,0:T(8,128)}, u32[]{:S(2)}) copy-start(f32[80,2560]{1,0:T(8,128)} %copy-done.2) | copy-start | bytes 2457604
  210.0 23.7 %all-to-all-start.2 = ((bf16[32,112,128]{2,1,0:T(8,128)(2,1)}), bf16[32,112,128]{2,1,0:T(8,128)(2,1)S(1)}, u32[]{:S(2)}, u32[]{:S(2)}) async-start(bf16[32,112,128]{2,1,0:T(8,128)(2,1)} %bitcast.25), calls=%async_computation.2 | async-start | bytes 1835008 | tf_op jit(solution)/shard_map/all_to_all | solution.py:429
  214.1 19.6 %collective-permute-start.3 = (bf16[80,2560]{1,0:T(8,128)(2,1)S(1)}, bf16[80,2560]{1,0:T(8,128)(2,1)S(1)}, u32[]{:S(2)}, u32[]{:S(2)}) collective-permute-start(bf16[80,2560]{1,0:T(8,128)(2,1)S(1)} %copy-done.8), channel_id=1, source_target_pairs={{0,64},{64,0},{1,65},{65,1},{2,66},{66,2},{3,67},{67,3},{4,68},{68... | collective-permute-start | bytes 1228808 | tf_op jit(solution)/shard_map/ppermute | solution.py:318
Sparse Core Ops, SparseCore 0:
  23.9 101.8 all-gather.2
